TPU v7x, 128 devices: a whole 4x4x4 slice. The times are simulated.
128 devices in a mesh: gx: 16 (over y, z), gy: 8 (over x, core).
Axes of the slice: x: 4, y: 4, z: 4, core: 2. Of those that a mesh axis runs over, the one named last changes fastest.
Arguments:
- fields: float32 [256, 64, 1536], P('gx', 'gy'), may hold values from -6 to 6
- resid: float32 [256, 64, 1536], P('gx', 'gy'), may hold values from -3 to 3
- permit: float32 [256, 64, 256], P('gx', 'gy'), may hold values from 1 to 8
- metric: float32 [256, 64, 768], P('gx', 'gy'), may hold values from 0.5 to 2
- route: int32 [16, 1024], P('gx', 'gy'), may hold values from 0 to 127, as said below
- stencil: int32 [1024, 1024], P('gx', 'gy'), may hold values from 0 to 255, as said below
- coords: float32 [2, 1024, 1024], P(None, 'gx', 'gy'), may hold values from -1 to 1
Outputs:
- fields_out: float32 [256, 64, 1536], P('gx', 'gy')
- resid_out: float32 [256, 64, 1536], P('gx', 'gy')
- plane: float32 [12, 1024, 1024], P(None, 'gx', 'gy')
Inputs may be any that keep to these rules, and one draw needn't show every extreme that they name: `route`: of the 128 columns of one partition, at most 2 have the same tile, and some tile has exactly 2 of them in every partition; every tile is the tile of exactly 128 columns in all. stencil[p, q] = s * 2 + r where r is below the number of columns of partition s whose tile is the pixel's tile.
All inputs are finite; a program needn't handle non-finite values.
Results may differ from a plain program's by a relative error of at most 0.0001.
Values sent between devices are 32-bit elements; how exact they have to be, the bound alone decides.
A program may use at most 128 MiB of HBM per device.

v0:
```python
import functools

import jax
import jax.numpy as jnp
import numpy as np
from jax import lax
from jax.experimental import pallas as pl
from jax.experimental.pallas import tpu as pltpu
from jax.sharding import PartitionSpec as P

section_decay = (-0.41789047449985195, -1.192151694642677)
section_gain = (0.37921031299962726, 0.8229550293869817)
time_step = 0.05
lift_factor = 3.0

MESH = pl.DeviceIdType.MESH
F32 = jnp.float32
BF16 = jnp.bfloat16
NX, NY = 16, 8
CH = 16


def gll_points():
    return np.array([-1.0, -np.sqrt(0.2), np.sqrt(0.2), 1.0])


def derivative_table():
    points = gll_points()
    barycentric = np.array(
        [1.0 / np.prod([points[j] - points[k] for k in range(4) if k != j]) for j in range(4)]
    )
    table = np.zeros((4, 4))
    for i in range(4):
        for j in range(4):
            if i != j:
                table[i, j] = barycentric[j] / barycentric[i] / (points[i] - points[j])
        table[i, i] = -np.sum(table[i])
    return table


def stacked_tables():
    table = derivative_table()
    table[3, 3] -= lift_factor
    table[0, 0] += lift_factor
    eye = np.eye(4)
    along = [
        np.kron(np.kron(table, eye), eye),
        np.kron(np.kron(eye, table), eye),
        np.kron(np.kron(eye, eye), table),
    ]
    two = [np.kron(np.eye(2), m).T for m in along]
    full = np.stack(
        [np.concatenate([two[(g + 1) % 3], two[(g + 2) % 3]], axis=1) for g in range(3)]
    ).astype(np.float32)
    high = full.astype(jnp.bfloat16)
    low = (full - high.astype(np.float32)).astype(jnp.bfloat16)
    return np.concatenate([high, high], axis=1), low


def lane_iota(rows):
    return lax.broadcasted_iota(jnp.int32, (rows, 128), 1)


def node_digit(axis, lane):
    return (lane >> (4 - 2 * axis)) & 3


def basis(coord):
    points = gll_points()
    listing = []
    for j in range(4):
        result = None
        for k in range(4):
            if k != j:
                term = (coord - float(points[k])) * float(1.0 / (points[j] - points[k]))
                result = term if result is None else result * term
        listing.append(result)
    return listing


def split2(value):
    high = value.astype(BF16)
    return high, (value - high.astype(F32)).astype(BF16)


def kernel(
    f_in, r_in, p_in, m_in, rt_in, st_in, co_in, w1_in, w2_in,
    f_out, r_out, pl_out,
    u, r, ep, me, rt, st, co, w1, w2,
    gxb, gyb, hys, hyr, qz, xs, rr, pay, og, b1, b2, tb, tt, oh, wt, pls,
    in_sem, out_sem, hs_sem, hr_sem, s1_sem, r1_sem, s2_sem, r2_sem,
):
    ix = lax.axis_index("gx")
    iy = lax.axis_index("gy")

    loads = [
        pltpu.make_async_copy(src, dst, in_sem.at[n])
        for n, (src, dst) in enumerate(
            [(f_in, u), (rt_in, rt), (w1_in, w1), (w2_in, w2), (m_in, me), (r_in, r),
             (p_in, ep), (st_in, st), (co_in, co)]
        )
    ]
    for load in loads:
        load.start()

    barrier = pltpu.get_barrier_semaphore()

    def greet_x(d, carry):
        pl.semaphore_signal(barrier, inc=1, device_id=(lax.rem(ix + d, NX), iy), device_id_type=MESH)
        return carry

    def greet_y(d, carry):
        pl.semaphore_signal(barrier, inc=1, device_id=(ix, lax.rem(iy + d, NY)), device_id_type=MESH)
        return carry

    lax.fori_loop(1, NX, greet_x, 0)
    lax.fori_loop(1, NY, greet_y, 0)

    lane = lane_iota(CH)
    digit = [node_digit(a, lane) for a in range(3)]
    sg = [
        jnp.where(d == 3, 1.0, jnp.where(d == 0, -1.0, 0.0)).astype(F32) for d in digit
    ]
    bd3 = [jnp.where((d == 3) | (d == 0), lift_factor, 0.0).astype(F32) for d in digit]
    sg3 = [lift_factor * s for s in sg]
    swap = []
    for a in range(3):
        reach = 3 << (4 - 2 * a)
        base = lane if a < 2 else lane ^ 64
        swap.append(
            jnp.where(digit[a] == 0, base + reach, jnp.where(digit[a] == 3, base - reach, lane))
        )
    is3 = [digit[0] == 3, digit[1] == 3]
    low_bottom = (digit[2] == 0) & (lane < 64)
    high_top = (digit[2] == 3) & (lane >= 64)
    pick = 64 + 4 * (lane >> 3) + 3
    comp_lane = lane & 7

    def permute(value, index):
        return jnp.take_along_axis(value, index, axis=1)

    def faces(sec, r0, ee, hh):
        xt = pl.multiple_of(r0, CH)
        for a in range(3):
            b, c = (a + 1) % 3, (a + 2) % 3
            for pair in range(2):
                sums, moved = [], []
                for lp in range(2):
                    if pair == 0:
                        t = ee[lp][b] + sg[a] * hh[lp][c]
                    else:
                        t = ee[lp][c] - sg[a] * hh[lp][b]
                    sums.append(t)
                    moved.append(permute(t, swap[a]))
                for lp in range(2):
                    k = pair * 2 + lp
                    if a == 0:
                        gxb[sec, k, pl.ds(xt + 8, CH), :] = moved[lp]
                    elif a == 1:
                        gyb[sec, k, pl.ds(2 * xt + 8, 8), :] = moved[lp][0:8]
                        gyb[sec, k, pl.ds(2 * xt + 24, 8), :] = moved[lp][8:16]
                    elif lp == 0:
                        qz[k, pl.ds(xt, CH), :] = jnp.where(
                            low_bottom, -sums[0], jnp.where(high_top, moved[1], moved[0])
                        )
                    else:
                        qz[k, pl.ds(xt, CH), :] = jnp.where(
                            high_top, 0.0, jnp.where(low_bottom, moved[0], moved[1])
                        )
        for g in range(3):
            for e, side in enumerate((ee, hh)):
                for lp in range(2):
                    high, low = split2(side[lp][g])
                    rows = pl.ds((e * 2 + lp) * 128 + xt, CH)
                    xs[g, rows, 0:128] = high
                    xs[g, rows, 128:256] = low

    def trace_rows(r0, ee, hh):
        total = jnp.zeros((CH, 128), F32)
        for c in range(6):
            side = ee if c < 3 else hh
            total = jnp.where(comp_lane == c, permute(side[1][c % 3], pick), total)
        pay[pl.ds(r0, CH), :] = total

    def tiles(ref, r0):
        return [
            [ref[pl.ds(r0, CH), (c * 2 + lp) * 128 : (c * 2 + lp + 1) * 128] for c in range(6)]
            for lp in range(2)
        ]

    def halo_copies(sec):
        below = {"x": lax.rem(ix + NX - 1, NX), "y": lax.rem(iy + NY - 1, NY)}
        above = {"x": lax.rem(ix + 1, NX), "y": lax.rem(iy + 1, NY)}
        plan = [
            (gxb.at[sec, :, pl.ds(8, 8)], gxb.at[sec, :, pl.ds(136, 8)], (below["x"], iy)),
            (gxb.at[sec, :, pl.ds(128, 8)], gxb.at[sec, :, pl.ds(0, 8)], (above["x"], iy)),
            (hys.at[sec, 0], hyr.at[sec, 0], (ix, below["y"])),
            (hys.at[sec, 1], hyr.at[sec, 1], (ix, above["y"])),
        ]
        return [
            pltpu.make_async_remote_copy(
                src_ref=src, dst_ref=dst, send_sem=hs_sem.at[sec, n], recv_sem=hr_sem.at[sec, n],
                device_id=device, device_id_type=MESH,
            )
            for n, (src, dst, device) in enumerate(plan)
        ]

    def send_halo(sec):
        for k in range(4):
            hys[sec, 0, k] = gyb[sec, k, pl.ds(8, 16, stride=16), :]
            hys[sec, 1, k] = gyb[sec, k, pl.ds(15, 16, stride=16), :]
        for copy in halo_copies(sec):
            copy.start()

    def take_halo(sec):
        for copy in halo_copies(sec):
            copy.wait_recv()

        @pl.when(ix == NX - 1)
        def _():
            gxb[sec, :, 136:144, :] = jnp.zeros((4, 8, 128), F32)

        @pl.when(ix == 0)
        def _():
            gxb[sec, :, 0:8, :] = jnp.zeros((4, 8, 128), F32)

        has_up = jnp.where(iy == NY - 1, 0.0, 1.0).astype(F32)
        has_down = jnp.where(iy == 0, 0.0, 1.0).astype(F32)
        for k in range(4):
            gyb[sec, k, pl.ds(16, 16, stride=16), :] = hyr[sec, 0, k] * has_up
            gyb[sec, k, pl.ds(7, 16, stride=16), :] = hyr[sec, 1, k] * has_down

    def products():
        def one(g, carry):
            rr[g] = jnp.dot(xs[g], w1[g], preferred_element_type=F32) + jnp.dot(
                xs[g, :, 0:128], w2[g], preferred_element_type=F32
            )
            return carry

        lax.fori_loop(0, 3, one, 0)

    def finish(sec, r0):
        xt = pl.multiple_of(r0, CH)
        rows = pl.ds(xt, CH)
        new = [[None] * 6, [None] * 6]
        for lp in range(2):
            cols = [slice((c * 2 + lp) * 128, (c * 2 + lp + 1) * 128) for c in range(6)]
            val = [u[rows, cols[c]] for c in range(6)]
            tend = [None] * 6

            def add(c, term):
                tend[c] = term if tend[c] is None else tend[c] + term

            def slope(comp, axis):
                g, e = comp % 3, comp // 3
                half = 0 if axis == (g + 1) % 3 else 1
                return rr[g, pl.ds((e * 2 + lp) * 128 + xt, CH), half * 128 : half * 128 + 128]

            for a in range(3):
                b, c = (a + 1) % 3, (a + 2) % 3
                met = me[rows, (a * 2 + lp) * 128 : (a * 2 + lp + 1) * 128]
                q = []
                for pair in range(2):
                    k = pair * 2 + lp
                    if a == 0:
                        q.append(
                            jnp.where(
                                is3[0],
                                gxb[sec, k, pl.ds(xt + 16, CH), :],
                                gxb[sec, k, pl.ds(xt, CH), :],
                            )
                        )
                    elif a == 1:
                        up = jnp.concatenate(
                            [gyb[sec, k, pl.ds(2 * xt + 9, 8), :], gyb[sec, k, pl.ds(2 * xt + 25, 8), :]],
                            axis=0,
                        )
                        down = jnp.concatenate(
                            [gyb[sec, k, pl.ds(2 * xt + 7, 8), :], gyb[sec, k, pl.ds(2 * xt + 23, 8), :]],
                            axis=0,
                        )
                        q.append(jnp.where(is3[1], up, down))
                    else:
                        q.append(qz[k, rows, :])
                add(b, met * (bd3[a] * (q[0] - val[b]) - slope(c + 3, a)))
                add(c + 3, met * (-(sg3[a] * q[0]) - bd3[a] * val[c + 3] - slope(b, a)))
                add(c, met * (bd3[a] * (q[1] - val[c]) + slope(b + 3, a)))
                add(b + 3, met * (sg3[a] * q[1] - bd3[a] * val[b + 3] + slope(c, a)))
            scale = time_step / ep[rows, lp * 128 : (lp + 1) * 128]
            for c in range(6):
                rate = tend[c] * scale if c < 3 else tend[c] * time_step
                reg = section_decay[sec] * r[rows, cols[c]] + rate
                r[rows, cols[c]] = reg
                value = val[c] + section_gain[sec] * reg
                u[rows, cols[c]] = value
                new[lp][c] = value
        return new

    def stage1(sample):
        def make(d):
            peer = lax.rem(ix + d, NX)
            return pltpu.make_async_remote_copy(
                src_ref=og.at[sample, pl.ds(pl.multiple_of(peer * 16, 16), 16)],
                dst_ref=b1.at[sample, pl.ds(pl.multiple_of(ix * 16, 16), 16)],
                send_sem=s1_sem.at[sample, d], recv_sem=r1_sem.at[sample, d],
                device_id=(peer, iy), device_id_type=MESH,
            )
        return make

    def stage2(sample):
        def make(d):
            peer = lax.rem(iy + d, NY)
            return pltpu.make_async_remote_copy(
                src_ref=b2.at[sample, pl.ds(pl.multiple_of(peer * 32, 32), 32)],
                dst_ref=tb.at[sample, pl.ds(pl.multiple_of(iy * 32, 32), 32)],
                send_sem=s2_sem.at[sample, d], recv_sem=r2_sem.at[sample, d],
                device_id=(ix, peer), device_id_type=MESH,
            )
        return make

    def each(count, make, act):
        def body(d, carry):
            act(make(d))
            return carry

        lax.fori_loop(1, count, body, 0)

    def place(sample):
        value = pay[...]
        high, rest = value.astype(BF16), None
        rest = value - high.astype(F32)
        mid = rest.astype(BF16)
        low = (rest - mid.astype(F32)).astype(BF16)
        slot = jnp.broadcast_to(slots, (256, 128))
        where = lax.broadcasted_iota(jnp.int32, (256, 128), 0) == slot
        put = jnp.where(where, 1.0, 0.0).astype(BF16)
        og[sample] = (
            jnp.dot(put, high, preferred_element_type=F32)
            + jnp.dot(put, mid, preferred_element_type=F32)
        ) + jnp.dot(put, low, preferred_element_type=F32)
        own = pl.ds(pl.multiple_of(ix * 16, 16), 16)
        b1[sample, own, :] = og[sample, own, :]

    def forward(sample):
        each(NX, stage1(sample), lambda copy: copy.wait_recv())
        for g in range(NY):
            for side in range(2):
                b2[sample, pl.ds(g * 32 + side * 16, 16), :] = b1[
                    sample, pl.ds(g * 2 + side, 16, stride=16), :
                ]
        own = pl.ds(pl.multiple_of(iy * 32, 32), 32)
        tb[sample, own, :] = b2[sample, own, :]
        each(NY, stage2(sample), lambda copy: copy.start())

    def interpolate(sample):
        each(NY, stage2(sample), lambda copy: copy.wait_recv())
        high, low = split2(tb[sample].T)
        tt[0:128] = high
        tt[128:256] = low

        def rows_of(pp, carry):
            got = jnp.dot(tt[...], oh[pp], preferred_element_type=F32)
            for h in range(2):
                part = got[:, h * 128 : h * 128 + 128]
                total = None
                for n in range(16):
                    both = part[n * 8 : n * 8 + 8] + part[128 + n * 8 : 136 + n * 8]
                    term = both * wt[n, pl.ds(2 * pp + h, 1), :]
                    total = term if total is None else total + term
                pls[pl.ds(sample * 512 + 2 * pp + h, 8, stride=64), :] = total
            return carry

        lax.fori_loop(0, 32, rows_of, 0)

    loads[0].wait()
    loads[1].wait()

    def first_faces(ch, carry):
        r0 = ch * CH
        both = tiles(u, pl.multiple_of(r0, CH))
        ee = [both[lp][0:3] for lp in range(2)]
        hh = [both[lp][3:6] for lp in range(2)]
        faces(0, r0, ee, hh)
        trace_rows(pl.multiple_of(r0, CH), ee, hh)
        return carry

    lax.fori_loop(0, 128 // CH, first_faces, 0)

    targets = jnp.broadcast_to(rt[...], (128, 128))
    earlier = lax.broadcasted_iota(jnp.int32, (128, 128), 0) < lane_iota(128)
    same = jnp.where((targets.T == targets) & earlier, 1, 0)
    slots = rt[...] * 2 + jnp.sum(same, axis=0, keepdims=True)

    pl.semaphore_wait(barrier, NX - 1 + NY - 1)
    send_halo(0)
    place(0)
    each(NX, stage1(0), lambda copy: copy.start())

    loads[2].wait()
    loads[3].wait()
    products()

    for load in loads[4:]:
        load.wait()

    stv = st[...]
    slot_of = ((stv >> 1) & 7) * 32 + (stv & 1) * 16 + (stv >> 4)
    st[...] = slot_of
    along_u = basis(co[0])
    along_v = basis(co[1])
    for i in range(4):
        for j in range(4):
            wt[i * 4 + j] = along_u[i] * along_v[j]
    slot_iota = lax.broadcasted_iota(jnp.int32, (256, 128), 0)

    def one_hot(pp, carry):
        for h in range(2):
            row = jnp.broadcast_to(st[pl.ds(2 * pp + h, 1), :], (256, 128))
            oh[pp, :, h * 128 : h * 128 + 128] = jnp.where(slot_iota == row, 1.0, 0.0).astype(BF16)
        return carry

    lax.fori_loop(0, 32, one_hot, 0)

    take_halo(0)

    def first_section(ch, carry):
        r0 = ch * CH
        new = finish(0, r0)
        ee = [new[lp][0:3] for lp in range(2)]
        hh = [new[lp][3:6] for lp in range(2)]
        faces(1, r0, ee, hh)
        trace_rows(pl.multiple_of(r0, CH), ee, hh)
        return carry

    lax.fori_loop(0, 128 // CH, first_section, 0)
    send_halo(1)
    place(1)
    each(NX, stage1(1), lambda copy: copy.start())
    forward(0)
    products()
    forward(1)
    take_halo(1)

    def second_section(ch, carry):
        finish(1, ch * CH)
        return carry

    lax.fori_loop(0, 128 // CH, second_section, 0)
    stores = [
        pltpu.make_async_copy(u, f_out, out_sem.at[0]),
        pltpu.make_async_copy(r, r_out, out_sem.at[1]),
        pltpu.make_async_copy(pls.at[pl.ds(0, 384)], pl_out.at[pl.ds(0, 384)], out_sem.at[2]),
        pltpu.make_async_copy(pls.at[pl.ds(512, 384)], pl_out.at[pl.ds(384, 384)], out_sem.at[3]),
    ]
    stores[0].start()
    stores[1].start()
    interpolate(0)
    stores[2].start()
    interpolate(1)
    stores[3].start()
    for sec in range(2):
        for copy in halo_copies(sec):
            copy.wait_send()
        each(NX, stage1(sec), lambda copy: copy.wait_send())
        each(NY, stage2(sec), lambda copy: copy.wait_send())
    for store in stores:
        store.wait()


def on_device(fields, resid, permit, metric, route, stencil, coords):
    columns = fields.shape[0] * fields.shape[1]
    w1, w2 = stacked_tables()
    anywhere = pl.BlockSpec(memory_space=pl.ANY)
    dma = pltpu.SemaphoreType.DMA
    f_out, r_out, plane = pl.pallas_call(
        kernel,
        out_shape=(
            jax.ShapeDtypeStruct((columns, 1536), F32),
            jax.ShapeDtypeStruct((columns, 1536), F32),
            jax.ShapeDtypeStruct((768, 128), F32),
        ),
        in_specs=[anywhere] * 9,
        out_specs=(anywhere,) * 3,
        scratch_shapes=[
            pltpu.VMEM((128, 1536), F32),
            pltpu.VMEM((128, 1536), F32),
            pltpu.VMEM((128, 256), F32),
            pltpu.VMEM((128, 768), F32),
            pltpu.VMEM((1, 128), jnp.int32),
            pltpu.VMEM((64, 128), jnp.int32),
            pltpu.VMEM((2, 64, 128), F32),
            pltpu.VMEM((3, 256, 256), BF16),
            pltpu.VMEM((3, 128, 256), BF16),
            pltpu.VMEM((2, 4, 144, 128), F32),
            pltpu.VMEM((2, 4, 272, 128), F32),
            pltpu.VMEM((2, 2, 4, 16, 128), F32),
            pltpu.VMEM((2, 2, 4, 16, 128), F32),
            pltpu.VMEM((4, 128, 128), F32),
            pltpu.VMEM((3, 512, 256), BF16),
            pltpu.VMEM((3, 512, 256), F32),
            pltpu.VMEM((128, 128), F32),
            pltpu.VMEM((2, 256, 128), F32),
            pltpu.VMEM((2, 256, 128), F32),
            pltpu.VMEM((2, 256, 128), F32),
            pltpu.VMEM((2, 256, 128), F32),
            pltpu.VMEM((256, 256), BF16),
            pltpu.VMEM((32, 256, 256), BF16),
            pltpu.VMEM((16, 64, 128), F32),
            pltpu.VMEM((1024, 128), F32),
            dma((9,)),
            dma((4,)),
            dma((2, 4)),
            dma((2, 4)),
            dma((2, NX)),
            dma((2, NX)),
            dma((2, NY)),
            dma((2, NY)),
        ],
        compiler_params=pltpu.CompilerParams(
            collective_id=0, has_side_effects=True, vmem_limit_bytes=40 * 1024 * 1024
        ),
    )(
        fields.reshape(columns, 1536),
        resid.reshape(columns, 1536),
        permit.reshape(columns, 256),
        metric.reshape(columns, 768),
        route,
        stencil,
        coords,
        jnp.asarray(w1),
        jnp.asarray(w2),
    )
    return (
        f_out.reshape(fields.shape),
        r_out.reshape(fields.shape),
        plane.reshape(12, stencil.shape[0], stencil.shape[1]),
    )


def solution(mesh):
    return jax.shard_map(
        on_device,
        mesh=mesh,
        in_specs=(
            P("gx", "gy", None),
            P("gx", "gy", None),
            P("gx", "gy", None),
            P("gx", "gy", None),
            P("gx", "gy"),
            P("gx", "gy"),
            P(None, "gx", "gy"),
        ),
        out_specs=(P("gx", "gy", None), P("gx", "gy", None), P(None, "gx", "gy")),
        check_vma=False,
    )
```

profile of v0, /device:TPU:1, one launch (start us, length us, event | category | flops | bytes accessed | tf_op | source)
XLA Modules:
  0.0 45.7 jit_solution(15596400356896795450)
XLA Ops:
  0.6 0.0 copy-start.8
  0.6 0.6 %copy-done.8 = s32[1,128]{1,0:T(1,128)S(1)} copy-done((s32[1,128]{1,0:T(1,128)S(1)}, s32[1,128]{1,0:T(1,128)}, u32[]{:S(2)}) %copy-start.8) | copy-done | bytes 536
  1.3 0.0 copy-start
  1.3 1.1 %copy-done = f32[16,8,1536]{2,1,0:T(8,128)S(1)} copy-done((f32[16,8,1536]{2,1,0:T(8,128)S(1)}, f32[16,8,1536]{2,1,0:T(8,128)}, u32[]{:S(2)}) %copy-start) | copy-done | bytes 786456
  2.4 0.0 copy-start.1
  2.4 1.1 %copy-done.1 = f32[16,8,1536]{2,1,0:T(8,128)S(1)} copy-done((f32[16,8,1536]{2,1,0:T(8,128)S(1)}, f32[16,8,1536]{2,1,0:T(8,128)}, u32[]{:S(2)}) %copy-start.1) | copy-done | bytes 786456
  3.6 0.0 copy-start.2
  3.6 1.0 %copy-done.2 = f32[16,8,768]{2,1,0:T(8,128)S(1)} copy-done((f32[16,8,768]{2,1,0:T(8,128)S(1)}, f32[16,8,768]{2,1,0:T(8,128)}, u32[]{:S(2)}) %copy-start.2) | copy-done | bytes 393240
  4.6 0.0 copy-start.3
  4.6 1.0 %copy-done.3 = bf16[3,256,256]{2,1,0:T(8,128)(2,1)S(1)} copy-done((bf16[3,256,256]{2,1,0:T(8,128)(2,1)S(1)}, bf16[3,256,256]{2,1,0:T(8,128)(2,1)}, u32[]{:S(2)}) %copy-start.3) | copy-done | bytes 393240
  5.5 0.0 copy-start.4
  5.6 0.9 %copy-done.4 = bf16[3,128,256]{2,1,0:T(8,128)(2,1)S(1)} copy-done((bf16[3,128,256]{2,1,0:T(8,128)(2,1)S(1)}, bf16[3,128,256]{2,1,0:T(8,128)(2,1)}, u32[]{:S(2)}) %copy-start.4) | copy-done | bytes 196632
  6.5 0.0 copy-start.5
  6.5 0.9 %copy-done.5 = f32[16,8,256]{2,1,0:T(8,128)S(1)} copy-done((f32[16,8,256]{2,1,0:T(8,128)S(1)}, f32[16,8,256]{2,1,0:T(8,128)}, u32[]{:S(2)}) %copy-start.5) | copy-done | bytes 131096
  7.4 0.0 copy-start.6
  7.4 0.8 %copy-done.6 = f32[2,64,128]{2,1,0:T(8,128)S(1)} copy-done((f32[2,64,128]{2,1,0:T(8,128)S(1)}, f32[2,64,128]{2,1,0:T(8,128)}, u32[]{:S(2)}) %copy-start.6) | copy-done | bytes 65560
  8.2 0.0 copy-start.7
  8.2 0.8 %copy-done.7 = s32[64,128]{1,0:T(8,128)S(1)} copy-done((s32[64,128]{1,0:T(8,128)S(1)}, s32[64,128]{1,0:T(8,128)}, u32[]{:S(2)}) %copy-start.7) | copy-done | bytes 32792
  9.0 34.2 %shard_map.112 = (f32[128,1536]{1,0:T(8,128)S(1)}, f32[128,1536]{1,0:T(8,128)S(1)}, f32[768,128]{1,0:T(8,128)S(1)}) custom-call(f32[128,1536]{1,0:T(8,128)S(1)} %bitcast.9, f32[128,1536]{1,0:T(8,128)S(1)} %bitcast.10, f32[128,256]{1,0:T(8,128)S(1)} %bitcast.13, f32[128,768]{1,0:T(8,128)S(1)} %bitcast.11, s32[1,128]{1,0:T(1,128)S(1)} %copy-done.8, ...), custom_call_target="tpu_custom_call" | custom-call | tf_op jit(solution)/shard_map/pallas_call | solution.py:475
  43.2 0.9 %copy.15 = f32[16,8,1536]{2,1,0:T(8,128)} copy(f32[16,8,1536]{2,1,0:T(8,128)S(1)} %bitcast.8) | data formatting | bytes 1572864
  44.1 0.9 %copy.16 = f32[16,8,1536]{2,1,0:T(8,128)} copy(f32[16,8,1536]{2,1,0:T(8,128)S(1)} %bitcast.7) | data formatting | bytes 1572864
  45.0 0.7 %copy.17 = f32[12,64,128]{2,1,0:T(8,128)} copy(f32[12,64,128]{2,1,0:T(8,128)S(1)} %bitcast.12) | data formatting | bytes 786432
Async XLA Ops:
  0.6 0.7 %copy-start.8 = (s32[1,128]{1,0:T(1,128)S(1)}, s32[1,128]{1,0:T(1,128)}, u32[]{:S(2)}) copy-start(s32[1,128]{1,0:T(1,128)} %rt_in.1) | copy-start | bytes 1540
  1.3 1.1 %copy-start = (f32[16,8,1536]{2,1,0:T(8,128)S(1)}, f32[16,8,1536]{2,1,0:T(8,128)}, u32[]{:S(2)}) copy-start(f32[16,8,1536]{2,1,0:T(8,128)} %param.9) | copy-start | bytes 2359300
  2.4 1.1 %copy-start.1 = (f32[16,8,1536]{2,1,0:T(8,128)S(1)}, f32[16,8,1536]{2,1,0:T(8,128)}, u32[]{:S(2)}) copy-start(f32[16,8,1536]{2,1,0:T(8,128)} %param.10) | copy-start | bytes 2359300
  3.6 1.0 %copy-start.2 = (f32[16,8,768]{2,1,0:T(8,128)S(1)}, f32[16,8,768]{2,1,0:T(8,128)}, u32[]{:S(2)}) copy-start(f32[16,8,768]{2,1,0:T(8,128)} %param.12) | copy-start | bytes 1179652
  4.6 1.0 %copy-start.3 = (bf16[3,256,256]{2,1,0:T(8,128)(2,1)S(1)}, bf16[3,256,256]{2,1,0:T(8,128)(2,1)}, u32[]{:S(2)}) copy-start(bf16[3,256,256]{2,1,0:T(8,128)(2,1)} %constant.4.clone.w1_in) | copy-start | bytes 1179652
  5.5 0.9 %copy-start.4 = (bf16[3,128,256]{2,1,0:T(8,128)(2,1)S(1)}, bf16[3,128,256]{2,1,0:T(8,128)(2,1)}, u32[]{:S(2)}) copy-start(bf16[3,128,256]{2,1,0:T(8,128)(2,1)} %constant.5.clone.w2_in) | copy-start | bytes 589828
  6.5 0.9 %copy-start.5 = (f32[16,8,256]{2,1,0:T(8,128)S(1)}, f32[16,8,256]{2,1,0:T(8,128)}, u32[]{:S(2)}) copy-start(f32[16,8,256]{2,1,0:T(8,128)} %param.11) | copy-start | bytes 393220
  7.4 0.8 %copy-start.6 = (f32[2,64,128]{2,1,0:T(8,128)S(1)}, f32[2,64,128]{2,1,0:T(8,128)}, u32[]{:S(2)}) copy-start(f32[2,64,128]{2,1,0:T(8,128)} %co_in.1) | copy-start | bytes 196612
  8.2 0.8 %copy-start.7 = (s32[64,128]{1,0:T(8,128)S(1)}, s32[64,128]{1,0:T(8,128)}, u32[]{:S(2)}) copy-start(s32[64,128]{1,0:T(8,128)} %st_in.1) | copy-start | bytes 98308
where the time goes:
time: 46.2 us; the launch traced here: 45.7 us
  Pallas kernels  34.2 us (74%)
  local copies, waits for them, and re-layouts  10.8 us (23%)
  between operations  0.66 us (1%)
    pallas_call x1, Pallas kernels, on_device(): pl.pallas_call(kernel, out_shape=(jax.ShapeDtypeStruct((columns, 1536), F...  34.2 us
    unnamed x21, local copies, waits for them, and re-layouts  10.8 us

commit v1 on v0

--- a/solution.py
+++ b/solution.py
@@ -17,6 +17,7 @@
 F32 = jnp.float32
 BF16 = jnp.bfloat16
 NX, NY = 16, 8
+VMEM_A, VMEM_B = 54, 16
 CH = 16
 
 
@@ -83,13 +84,51 @@
     return high, (value - high.astype(F32)).astype(BF16)
 
 
+def interpolate(table, tt, oh, wt, pls):
+    high, low = split2(table.T)
+    tt[0:128] = high
+    tt[128:256] = low
+
+    def rows_of(pp, carry):
+        got = jnp.dot(tt[...], oh[pp], preferred_element_type=F32)
+        for h in range(2):
+            part = got[:, h * 128 : h * 128 + 128]
+            total = None
+            for n in range(16):
+                both = part[n * 8 : n * 8 + 8] + part[128 + n * 8 : 136 + n * 8]
+                term = both * wt[n, pl.ds(2 * pp + h, 1), :]
+                total = term if total is None else total + term
+            pls[pl.ds(2 * pp + h, 8, stride=64), :] = total
+        return carry
+
+    lax.fori_loop(0, 32, rows_of, 0, unroll=8)
+
+
+def last_kernel(
+    u, r, tb1, oh, wt, pls0, f_out, r_out, pl_out, pls1, tt, out_sem
+):
+    stores = [
+        pltpu.make_async_copy(u, f_out, out_sem.at[0]),
+        pltpu.make_async_copy(r, r_out, out_sem.at[1]),
+        pltpu.make_async_copy(pls0.at[pl.ds(0, 384)], pl_out.at[pl.ds(0, 384)], out_sem.at[2]),
+        pltpu.make_async_copy(pls1.at[pl.ds(0, 384)], pl_out.at[pl.ds(384, 384)], out_sem.at[3]),
+    ]
+    for store in stores[:3]:
+        store.start()
+    interpolate(tb1[...], tt, oh, wt, pls1)
+    stores[3].start()
+    for store in stores:
+        store.wait()
+
+
 def kernel(
     f_in, r_in, p_in, m_in, rt_in, st_in, co_in, w1_in, w2_in,
-    f_out, r_out, pl_out,
-    u, r, ep, me, rt, st, co, w1, w2,
-    gxb, gyb, hys, hyr, qz, xs, rr, pay, og, b1, b2, tb, tt, oh, wt, pls,
-    in_sem, out_sem, hs_sem, hr_sem, s1_sem, r1_sem, s2_sem, r2_sem,
+    u, r, tb1, oh, wt, pls,
+    ep, me, rt, st, co, w1, w2,
+    gxb, gyb, hys, hyr, qz, xs, rr, pay, og, b1, b2, tb0, tt,
+    in_sem, hs_sem, hr_sem, s1_sem, r1_sem, s2_sem, r2_sem,
 ):
+    tb = (tb0, tb1)
     ix = lax.axis_index("gx")
     iy = lax.axis_index("gy")
 
@@ -312,7 +351,7 @@
             peer = lax.rem(iy + d, NY)
             return pltpu.make_async_remote_copy(
                 src_ref=b2.at[sample, pl.ds(pl.multiple_of(peer * 32, 32), 32)],
-                dst_ref=tb.at[sample, pl.ds(pl.multiple_of(iy * 32, 32), 32)],
+                dst_ref=tb[sample].at[pl.ds(pl.multiple_of(iy * 32, 32), 32)],
                 send_sem=s2_sem.at[sample, d], recv_sem=r2_sem.at[sample, d],
                 device_id=(ix, peer), device_id_type=MESH,
             )
@@ -349,28 +388,8 @@
                     sample, pl.ds(g * 2 + side, 16, stride=16), :
                 ]
         own = pl.ds(pl.multiple_of(iy * 32, 32), 32)
-        tb[sample, own, :] = b2[sample, own, :]
+        tb[sample][own, :] = b2[sample, own, :]
         each(NY, stage2(sample), lambda copy: copy.start())
-
-    def interpolate(sample):
-        each(NY, stage2(sample), lambda copy: copy.wait_recv())
-        high, low = split2(tb[sample].T)
-        tt[0:128] = high
-        tt[128:256] = low
-
-        def rows_of(pp, carry):
-            got = jnp.dot(tt[...], oh[pp], preferred_element_type=F32)
-            for h in range(2):
-                part = got[:, h * 128 : h * 128 + 128]
-                total = None
-                for n in range(16):
-                    both = part[n * 8 : n * 8 + 8] + part[128 + n * 8 : 136 + n * 8]
-                    term = both * wt[n, pl.ds(2 * pp + h, 1), :]
-                    total = term if total is None else total + term
-                pls[pl.ds(sample * 512 + 2 * pp + h, 8, stride=64), :] = total
-            return carry
-
-        lax.fori_loop(0, 32, rows_of, 0)
 
     loads[0].wait()
     loads[1].wait()
@@ -421,6 +440,7 @@
 
     lax.fori_loop(0, 32, one_hot, 0)
 
+    forward(0)
     take_halo(0)
 
     def first_section(ch, carry):
@@ -436,8 +456,9 @@
     send_halo(1)
     place(1)
     each(NX, stage1(1), lambda copy: copy.start())
-    forward(0)
     products()
+    each(NY, stage2(0), lambda copy: copy.wait_recv())
+    interpolate(tb0[...], tt, oh, wt, pls)
     forward(1)
     take_halo(1)
 
@@ -446,44 +467,34 @@
         return carry
 
     lax.fori_loop(0, 128 // CH, second_section, 0)
-    stores = [
-        pltpu.make_async_copy(u, f_out, out_sem.at[0]),
-        pltpu.make_async_copy(r, r_out, out_sem.at[1]),
-        pltpu.make_async_copy(pls.at[pl.ds(0, 384)], pl_out.at[pl.ds(0, 384)], out_sem.at[2]),
-        pltpu.make_async_copy(pls.at[pl.ds(512, 384)], pl_out.at[pl.ds(384, 384)], out_sem.at[3]),
-    ]
-    stores[0].start()
-    stores[1].start()
-    interpolate(0)
-    stores[2].start()
-    interpolate(1)
-    stores[3].start()
+    each(NY, stage2(1), lambda copy: copy.wait_recv())
     for sec in range(2):
         for copy in halo_copies(sec):
             copy.wait_send()
         each(NX, stage1(sec), lambda copy: copy.wait_send())
         each(NY, stage2(sec), lambda copy: copy.wait_send())
-    for store in stores:
-        store.wait()
 
 
 def on_device(fields, resid, permit, metric, route, stencil, coords):
     columns = fields.shape[0] * fields.shape[1]
     w1, w2 = stacked_tables()
-    anywhere = pl.BlockSpec(memory_space=pl.ANY)
+    hbm = pl.BlockSpec(memory_space=pltpu.HBM)
+    vmem = pl.BlockSpec(memory_space=pltpu.VMEM)
     dma = pltpu.SemaphoreType.DMA
-    f_out, r_out, plane = pl.pallas_call(
+    kept = (
+        pltpu.VMEM((128, 1536), F32),
+        pltpu.VMEM((128, 1536), F32),
+        pltpu.VMEM((256, 128), F32),
+        pltpu.VMEM((32, 256, 256), BF16),
+        pltpu.VMEM((16, 64, 128), F32),
+        pltpu.VMEM((512, 128), F32),
+    )
+    held = pl.pallas_call(
         kernel,
-        out_shape=(
-            jax.ShapeDtypeStruct((columns, 1536), F32),
-            jax.ShapeDtypeStruct((columns, 1536), F32),
-            jax.ShapeDtypeStruct((768, 128), F32),
-        ),
-        in_specs=[anywhere] * 9,
-        out_specs=(anywhere,) * 3,
+        out_shape=kept,
+        in_specs=[hbm] * 9,
+        out_specs=(vmem,) * len(kept),
         scratch_shapes=[
-            pltpu.VMEM((128, 1536), F32),
-            pltpu.VMEM((128, 1536), F32),
             pltpu.VMEM((128, 256), F32),
             pltpu.VMEM((128, 768), F32),
             pltpu.VMEM((1, 128), jnp.int32),
@@ -502,13 +513,9 @@
             pltpu.VMEM((2, 256, 128), F32),
             pltpu.VMEM((2, 256, 128), F32),
             pltpu.VMEM((2, 256, 128), F32),
-            pltpu.VMEM((2, 256, 128), F32),
+            pltpu.VMEM((256, 128), F32),
             pltpu.VMEM((256, 256), BF16),
-            pltpu.VMEM((32, 256, 256), BF16),
-            pltpu.VMEM((16, 64, 128), F32),
-            pltpu.VMEM((1024, 128), F32),
             dma((9,)),
-            dma((4,)),
             dma((2, 4)),
             dma((2, 4)),
             dma((2, NX)),
@@ -517,7 +524,7 @@
             dma((2, NY)),
         ],
         compiler_params=pltpu.CompilerParams(
-            collective_id=0, has_side_effects=True, vmem_limit_bytes=40 * 1024 * 1024
+            collective_id=0, has_side_effects=True, vmem_limit_bytes=VMEM_A * 1024 * 1024
         ),
     )(
         fields.reshape(columns, 1536),
@@ -530,6 +537,18 @@
         jnp.asarray(w1),
         jnp.asarray(w2),
     )
+    f_out, r_out, plane = pl.pallas_call(
+        last_kernel,
+        out_shape=(
+            jax.ShapeDtypeStruct((columns, 1536), F32),
+            jax.ShapeDtypeStruct((columns, 1536), F32),
+            jax.ShapeDtypeStruct((768, 128), F32),
+        ),
+        in_specs=[vmem] * len(kept),
+        out_specs=(hbm,) * 3,
+        scratch_shapes=[pltpu.VMEM((512, 128), F32), pltpu.VMEM((256, 256), BF16), dma((4,))],
+        compiler_params=pltpu.CompilerParams(vmem_limit_bytes=VMEM_B * 1024 * 1024),
+    )(*held)
     return (
         f_out.reshape(fields.shape),
         r_out.reshape(fields.shape),

time: 46.2 us -> 30.2 us (0.65)
  local copies, waits for them, and re-layouts: 10.8 us -> 0 us
  Pallas kernels: 34.2 us -> 29.4 us
    unnamed x21 -> x0, local copies, waits for them, and re-layouts: 10.8 us -> none
    pallas_call x1 -> x2, Pallas kernels: 34.2 us -> 29.4 us  [the longest x1 26.8 us: on_device(): pl.pallas_call(kernel, out_shape=kept, in_specs=[hbm] * 9, out_specs=(vme...]
where the time goes in v1:
time: 30.2 us; the launch traced here: 30 us
  Pallas kernels  29.4 us (97%)
  between operations  0.64 us (2%)
    pallas_call x1, Pallas kernels, on_device(): pl.pallas_call(kernel, out_shape=kept, in_specs=[hbm] * 9, out_specs=(vme...  26.8 us
    pallas_call x1, Pallas kernels, on_device(): pl.pallas_call(last_kernel, out_shape=(jax.ShapeDtypeStruct((columns, 153...  2.62 us

profile of v1, /device:TPU:1, one launch (start us, length us, event | category | flops | bytes accessed | tf_op | source)
XLA Modules:
  0.0 30.0 jit_solution(14022461463443069319)
XLA Ops:
  0.6 26.8 %shard_map.112 = (f32[128,1536]{1,0:T(8,128)S(1)}, f32[128,1536]{1,0:T(8,128)S(1)}, f32[256,128]{1,0:T(8,128)S(1)}, bf16[32,256,256]{2,1,0:T(8,128)(2,1)S(1)}, f...) custom-call(f32[128,1536]{1,0:T(8,128)} %bitcast.7, f32[128,1536]{1,0:T(8,128)} %bitcast.8, f32[128,256]{1,0:T(8,128)} %bitcast.10, ...), custom_call_target="tpu_custom_call" | custom-call | tf_op jit(solution)/shard_map/pallas_call | solution.py:492
  27.4 2.6 %shard_map.113 = (f32[128,1536]{1,0:T(8,128)}, f32[128,1536]{1,0:T(8,128)}, f32[768,128]{1,0:T(8,128)}) custom-call(f32[128,1536]{1,0:T(8,128)S(1)} %get-tuple-element.12.u, f32[128,1536]{1,0:T(8,128)S(1)} %get-tuple-element.13.r, f32[256,128]{1,0:T(8,128)S(1)} %get-tuple-element.14.tb1, bf16[32,256,256]{2,1,0:T(8,128)(2,1)S(1)} %get-tuple-element.15.oh, ...), custom_call_target="tpu_custom_call" | custom-call | tf_op jit(solution)/shard_map/pallas_call | solution.py:540

commit v2 on v1

--- a/solution.py
+++ b/solution.py
@@ -125,10 +125,9 @@
     f_in, r_in, p_in, m_in, rt_in, st_in, co_in, w1_in, w2_in,
     u, r, tb1, oh, wt, pls,
     ep, me, rt, st, co, w1, w2,
-    gxb, gyb, hys, hyr, qz, xs, rr, pay, og, b1, b2, tb0, tt,
-    in_sem, hs_sem, hr_sem, s1_sem, r1_sem, s2_sem, r2_sem,
+    gxb, gyb, hys, hyr, qz, xs, rr, pay, og, b1, b2, tb0, nat, tt,
+    in_sem, hs_sem, hr_sem, s1_sem, r1_sem, s2_sem, r2_sem, sd_sem, rd_sem, ready,
 ):
-    tb = (tb0, tb1)
     ix = lax.axis_index("gx")
     iy = lax.axis_index("gy")
 
@@ -335,27 +334,42 @@
                 new[lp][c] = value
         return new
 
-    def stage1(sample):
-        def make(d):
-            peer = lax.rem(ix + d, NX)
-            return pltpu.make_async_remote_copy(
-                src_ref=og.at[sample, pl.ds(pl.multiple_of(peer * 16, 16), 16)],
-                dst_ref=b1.at[sample, pl.ds(pl.multiple_of(ix * 16, 16), 16)],
-                send_sem=s1_sem.at[sample, d], recv_sem=r1_sem.at[sample, d],
-                device_id=(peer, iy), device_id_type=MESH,
-            )
-        return make
-
-    def stage2(sample):
-        def make(d):
-            peer = lax.rem(iy + d, NY)
-            return pltpu.make_async_remote_copy(
-                src_ref=b2.at[sample, pl.ds(pl.multiple_of(peer * 32, 32), 32)],
-                dst_ref=tb[sample].at[pl.ds(pl.multiple_of(iy * 32, 32), 32)],
-                send_sem=s2_sem.at[sample, d], recv_sem=r2_sem.at[sample, d],
-                device_id=(ix, peer), device_id_type=MESH,
-            )
-        return make
+    def stage1(d):
+        peer = lax.rem(ix + d, NX)
+        return pltpu.make_async_remote_copy(
+            src_ref=og.at[0, pl.ds(pl.multiple_of(peer * 16, 16), 16)],
+            dst_ref=b1.at[pl.ds(pl.multiple_of(ix * 16, 16), 16)],
+            send_sem=s1_sem.at[d], recv_sem=r1_sem.at[d],
+            device_id=(peer, iy), device_id_type=MESH,
+        )
+
+    def stage2(d):
+        peer = lax.rem(iy + d, NY)
+        return pltpu.make_async_remote_copy(
+            src_ref=b2.at[pl.ds(pl.multiple_of(peer * 32, 32), 32)],
+            dst_ref=tb0.at[pl.ds(pl.multiple_of(iy * 32, 32), 32)],
+            send_sem=s2_sem.at[d], recv_sem=r2_sem.at[d],
+            device_id=(ix, peer), device_id_type=MESH,
+        )
+
+    me_flat = ix * NY + iy
+
+    def straight(d):
+        peer = lax.rem(me_flat + d, NX * NY)
+        return pltpu.make_async_remote_copy(
+            src_ref=og.at[1, pl.ds(peer * 2, 2)],
+            dst_ref=tb1.at[pl.ds(me_flat * 2, 2)],
+            send_sem=sd_sem, recv_sem=rd_sem,
+            device_id=(lax.div(peer, NY), lax.rem(peer, NY)), device_id_type=MESH,
+        )
+
+    def all_straight():
+        whole = pl.ds(0, 2 * (NX * NY - 1))
+        return pltpu.make_async_remote_copy(
+            src_ref=og.at[1, whole], dst_ref=tb1.at[whole],
+            send_sem=sd_sem, recv_sem=rd_sem,
+            device_id=(lax.rem(ix + 1, NX), iy), device_id_type=MESH,
+        )
 
     def each(count, make, act):
         def body(d, carry):
@@ -377,19 +391,22 @@
             jnp.dot(put, high, preferred_element_type=F32)
             + jnp.dot(put, mid, preferred_element_type=F32)
         ) + jnp.dot(put, low, preferred_element_type=F32)
-        own = pl.ds(pl.multiple_of(ix * 16, 16), 16)
-        b1[sample, own, :] = og[sample, own, :]
-
-    def forward(sample):
-        each(NX, stage1(sample), lambda copy: copy.wait_recv())
+
+    def forward():
+        each(NX, stage1, lambda copy: copy.wait_recv())
         for g in range(NY):
             for side in range(2):
-                b2[sample, pl.ds(g * 32 + side * 16, 16), :] = b1[
-                    sample, pl.ds(g * 2 + side, 16, stride=16), :
-                ]
+                b2[pl.ds(g * 32 + side * 16, 16), :] = b1[pl.ds(g * 2 + side, 16, stride=16), :]
         own = pl.ds(pl.multiple_of(iy * 32, 32), 32)
-        tb[sample][own, :] = b2[sample, own, :]
-        each(NY, stage2(sample), lambda copy: copy.start())
+        tb0[own, :] = b2[own, :]
+        each(NY, stage2, lambda copy: copy.start())
+
+    def gathered():
+        each(NY, stage2, lambda copy: copy.wait_recv())
+        for g in range(NY):
+            for side in range(2):
+                nat[pl.ds(g * 2 + side, 16, stride=16), :] = tb0[pl.ds(g * 32 + side * 16, 16), :]
+        return nat[...]
 
     loads[0].wait()
     loads[1].wait()
@@ -412,8 +429,16 @@
 
     pl.semaphore_wait(barrier, NX - 1 + NY - 1)
     send_halo(0)
+
+    def tell(d, carry):
+        pl.semaphore_signal(ready, inc=1, device_id=(ix, lax.rem(iy + d, NY)), device_id_type=MESH)
+        return carry
+
+    lax.fori_loop(1, NY, tell, 0)
     place(0)
-    each(NX, stage1(0), lambda copy: copy.start())
+    own = pl.ds(pl.multiple_of(ix * 16, 16), 16)
+    b1[own, :] = og[0, own, :]
+    each(NX, stage1, lambda copy: copy.start())
 
     loads[2].wait()
     loads[3].wait()
@@ -422,9 +447,6 @@
     for load in loads[4:]:
         load.wait()
 
-    stv = st[...]
-    slot_of = ((stv >> 1) & 7) * 32 + (stv & 1) * 16 + (stv >> 4)
-    st[...] = slot_of
     along_u = basis(co[0])
     along_v = basis(co[1])
     for i in range(4):
@@ -440,7 +462,6 @@
 
     lax.fori_loop(0, 32, one_hot, 0)
 
-    forward(0)
     take_halo(0)
 
     def first_section(ch, carry):
@@ -453,13 +474,14 @@
         return carry
 
     lax.fori_loop(0, 128 // CH, first_section, 0)
+    place(1)
+    pl.semaphore_wait(ready, NY - 1)
+    each(NX * NY, straight, lambda copy: copy.start())
     send_halo(1)
-    place(1)
-    each(NX, stage1(1), lambda copy: copy.start())
+    mine = pl.ds(me_flat * 2, 2)
+    tb1[mine, :] = og[1, mine, :]
+    forward()
     products()
-    each(NY, stage2(0), lambda copy: copy.wait_recv())
-    interpolate(tb0[...], tt, oh, wt, pls)
-    forward(1)
     take_halo(1)
 
     def second_section(ch, carry):
@@ -467,12 +489,14 @@
         return carry
 
     lax.fori_loop(0, 128 // CH, second_section, 0)
-    each(NY, stage2(1), lambda copy: copy.wait_recv())
+    interpolate(gathered(), tt, oh, wt, pls)
+    all_straight().wait_recv()
     for sec in range(2):
         for copy in halo_copies(sec):
             copy.wait_send()
-        each(NX, stage1(sec), lambda copy: copy.wait_send())
-        each(NY, stage2(sec), lambda copy: copy.wait_send())
+    each(NX, stage1, lambda copy: copy.wait_send())
+    each(NY, stage2, lambda copy: copy.wait_send())
+    all_straight().wait_send()
 
 
 def on_device(fields, resid, permit, metric, route, stencil, coords):
@@ -511,17 +535,21 @@
             pltpu.VMEM((3, 512, 256), F32),
             pltpu.VMEM((128, 128), F32),
             pltpu.VMEM((2, 256, 128), F32),
-            pltpu.VMEM((2, 256, 128), F32),
-            pltpu.VMEM((2, 256, 128), F32),
+            pltpu.VMEM((256, 128), F32),
+            pltpu.VMEM((256, 128), F32),
+            pltpu.VMEM((256, 128), F32),
             pltpu.VMEM((256, 128), F32),
             pltpu.VMEM((256, 256), BF16),
             dma((9,)),
             dma((2, 4)),
             dma((2, 4)),
-            dma((2, NX)),
-            dma((2, NX)),
-            dma((2, NY)),
-            dma((2, NY)),
+            dma((NX,)),
+            dma((NX,)),
+            dma((NY,)),
+            dma((NY,)),
+            dma,
+            dma,
+            pltpu.SemaphoreType.REGULAR,
         ],
         compiler_params=pltpu.CompilerParams(
             collective_id=0, has_side_effects=True, vmem_limit_bytes=VMEM_A * 1024 * 1024

time: 30.2 us -> 26.9 us (0.89)
  Pallas kernels: 29.4 us -> 26.1 us
    pallas_call x1, Pallas kernels: 26.8 us -> 23.5 us  [on_device(): pl.pallas_call(kernel, out_shape=kept, in_specs=[hbm] * 9, out_specs=(vme...]
where the time goes in v2:
time: 26.9 us; the launch traced here: 26.7 us
  Pallas kernels  26.1 us (97%)
  between operations  0.64 us (2%)
    pallas_call x1, Pallas kernels, on_device(): pl.pallas_call(kernel, out_shape=kept, in_specs=[hbm] * 9, out_specs=(vme...  23.5 us
    pallas_call x1, Pallas kernels, on_device(): pl.pallas_call(last_kernel, out_shape=(jax.ShapeDtypeStruct((columns, 153...  2.62 us

profile of v2, /device:TPU:1, one launch (start us, length us, event | category | flops | bytes accessed | tf_op | source)
XLA Modules:
  0.0 26.7 jit_solution(5411527837712104751)
XLA Ops:
  0.6 23.5 %shard_map.112 = (f32[128,1536]{1,0:T(8,128)S(1)}, f32[128,1536]{1,0:T(8,128)S(1)}, f32[256,128]{1,0:T(8,128)S(1)}, bf16[32,256,256]{2,1,0:T(8,128)(2,1)S(1)}, f...) custom-call(f32[128,1536]{1,0:T(8,128)} %bitcast.7, f32[128,1536]{1,0:T(8,128)} %bitcast.8, f32[128,256]{1,0:T(8,128)} %bitcast.10, ...), custom_call_target="tpu_custom_call" | custom-call | tf_op jit(solution)/shard_map/pallas_call | solution.py:516
  24.1 2.6 %shard_map.113 = (f32[128,1536]{1,0:T(8,128)}, f32[128,1536]{1,0:T(8,128)}, f32[768,128]{1,0:T(8,128)}) custom-call(f32[128,1536]{1,0:T(8,128)S(1)} %get-tuple-element.12.u, f32[128,1536]{1,0:T(8,128)S(1)} %get-tuple-element.13.r, f32[256,128]{1,0:T(8,128)S(1)} %get-tuple-element.14.tb1, bf16[32,256,256]{2,1,0:T(8,128)(2,1)S(1)} %get-tuple-element.15.oh, ...), custom_call_target="tpu_custom_call" | custom-call | tf_op jit(solution)/shard_map/pallas_call | solution.py:568

commit v3 on v1

--- a/solution.py
+++ b/solution.py
@@ -125,8 +125,8 @@
     f_in, r_in, p_in, m_in, rt_in, st_in, co_in, w1_in, w2_in,
     u, r, tb1, oh, wt, pls,
     ep, me, rt, st, co, w1, w2,
-    gxb, gyb, hys, hyr, qz, xs, rr, pay, og, b1, b2, tb0, tt,
-    in_sem, hs_sem, hr_sem, s1_sem, r1_sem, s2_sem, r2_sem,
+    gxb, gyb, hys, hyr, qz, xs, rr, pay, og, tb0, tt,
+    in_sem, hs_sem, hr_sem, sd_sem, rd_sem, ready,
 ):
     tb = (tb0, tb1)
     ix = lax.axis_index("gx")
@@ -335,27 +335,31 @@
                 new[lp][c] = value
         return new
 
-    def stage1(sample):
+    me_flat = ix * NY + iy
+
+    def straight(sample):
         def make(d):
-            peer = lax.rem(ix + d, NX)
+            peer = lax.rem(me_flat + d, NX * NY)
             return pltpu.make_async_remote_copy(
-                src_ref=og.at[sample, pl.ds(pl.multiple_of(peer * 16, 16), 16)],
-                dst_ref=b1.at[sample, pl.ds(pl.multiple_of(ix * 16, 16), 16)],
-                send_sem=s1_sem.at[sample, d], recv_sem=r1_sem.at[sample, d],
-                device_id=(peer, iy), device_id_type=MESH,
+                src_ref=og.at[sample, pl.ds(peer * 2, 2)],
+                dst_ref=tb[sample].at[pl.ds(me_flat * 2, 2)],
+                send_sem=sd_sem.at[sample], recv_sem=rd_sem.at[sample],
+                device_id=(lax.div(peer, NY), lax.rem(peer, NY)), device_id_type=MESH,
             )
         return make
 
-    def stage2(sample):
-        def make(d):
-            peer = lax.rem(iy + d, NY)
-            return pltpu.make_async_remote_copy(
-                src_ref=b2.at[sample, pl.ds(pl.multiple_of(peer * 32, 32), 32)],
-                dst_ref=tb[sample].at[pl.ds(pl.multiple_of(iy * 32, 32), 32)],
-                send_sem=s2_sem.at[sample, d], recv_sem=r2_sem.at[sample, d],
-                device_id=(ix, peer), device_id_type=MESH,
-            )
-        return make
+    def all_straight(sample):
+        whole = pl.ds(0, 2 * (NX * NY - 1))
+        return pltpu.make_async_remote_copy(
+            src_ref=og.at[sample, whole], dst_ref=tb[sample].at[whole],
+            send_sem=sd_sem.at[sample], recv_sem=rd_sem.at[sample],
+            device_id=(lax.rem(ix + 1, NX), iy), device_id_type=MESH,
+        )
+
+    def send_traces(sample):
+        each(NX * NY, straight(sample), lambda copy: copy.start())
+        mine = pl.ds(me_flat * 2, 2)
+        tb[sample][mine, :] = og[sample, mine, :]
 
     def each(count, make, act):
         def body(d, carry):
@@ -377,19 +381,6 @@
             jnp.dot(put, high, preferred_element_type=F32)
             + jnp.dot(put, mid, preferred_element_type=F32)
         ) + jnp.dot(put, low, preferred_element_type=F32)
-        own = pl.ds(pl.multiple_of(ix * 16, 16), 16)
-        b1[sample, own, :] = og[sample, own, :]
-
-    def forward(sample):
-        each(NX, stage1(sample), lambda copy: copy.wait_recv())
-        for g in range(NY):
-            for side in range(2):
-                b2[sample, pl.ds(g * 32 + side * 16, 16), :] = b1[
-                    sample, pl.ds(g * 2 + side, 16, stride=16), :
-                ]
-        own = pl.ds(pl.multiple_of(iy * 32, 32), 32)
-        tb[sample][own, :] = b2[sample, own, :]
-        each(NY, stage2(sample), lambda copy: copy.start())
 
     loads[0].wait()
     loads[1].wait()
@@ -412,8 +403,13 @@
 
     pl.semaphore_wait(barrier, NX - 1 + NY - 1)
     send_halo(0)
+
+    def tell(d, carry):
+        pl.semaphore_signal(ready, inc=1, device_id=(ix, lax.rem(iy + d, NY)), device_id_type=MESH)
+        return carry
+
+    lax.fori_loop(1, NY, tell, 0)
     place(0)
-    each(NX, stage1(0), lambda copy: copy.start())
 
     loads[2].wait()
     loads[3].wait()
@@ -422,9 +418,6 @@
     for load in loads[4:]:
         load.wait()
 
-    stv = st[...]
-    slot_of = ((stv >> 1) & 7) * 32 + (stv & 1) * 16 + (stv >> 4)
-    st[...] = slot_of
     along_u = basis(co[0])
     along_v = basis(co[1])
     for i in range(4):
@@ -440,7 +433,8 @@
 
     lax.fori_loop(0, 32, one_hot, 0)
 
-    forward(0)
+    pl.semaphore_wait(ready, NY - 1)
+    send_traces(0)
     take_halo(0)
 
     def first_section(ch, carry):
@@ -453,13 +447,12 @@
         return carry
 
     lax.fori_loop(0, 128 // CH, first_section, 0)
+    place(1)
+    send_traces(1)
     send_halo(1)
-    place(1)
-    each(NX, stage1(1), lambda copy: copy.start())
     products()
-    each(NY, stage2(0), lambda copy: copy.wait_recv())
+    all_straight(0).wait_recv()
     interpolate(tb0[...], tt, oh, wt, pls)
-    forward(1)
     take_halo(1)
 
     def second_section(ch, carry):
@@ -467,12 +460,11 @@
         return carry
 
     lax.fori_loop(0, 128 // CH, second_section, 0)
-    each(NY, stage2(1), lambda copy: copy.wait_recv())
+    all_straight(1).wait_recv()
     for sec in range(2):
         for copy in halo_copies(sec):
             copy.wait_send()
-        each(NX, stage1(sec), lambda copy: copy.wait_send())
-        each(NY, stage2(sec), lambda copy: copy.wait_send())
+        all_straight(sec).wait_send()
 
 
 def on_device(fields, resid, permit, metric, route, stencil, coords):
@@ -511,17 +503,14 @@
             pltpu.VMEM((3, 512, 256), F32),
             pltpu.VMEM((128, 128), F32),
             pltpu.VMEM((2, 256, 128), F32),
-            pltpu.VMEM((2, 256, 128), F32),
-            pltpu.VMEM((2, 256, 128), F32),
             pltpu.VMEM((256, 128), F32),
             pltpu.VMEM((256, 256), BF16),
             dma((9,)),
             dma((2, 4)),
             dma((2, 4)),
-            dma((2, NX)),
-            dma((2, NX)),
-            dma((2, NY)),
-            dma((2, NY)),
+            dma((2,)),
+            dma((2,)),
+            pltpu.SemaphoreType.REGULAR,
         ],
         compiler_params=pltpu.CompilerParams(
             collective_id=0, has_side_effects=True, vmem_limit_bytes=VMEM_A * 1024 * 1024

time: 30.2 us -> 24.5 us (0.81)
  Pallas kernels: 29.4 us -> 23.7 us
    pallas_call x1, Pallas kernels: 26.8 us -> 21.1 us  [on_device(): pl.pallas_call(kernel, out_shape=kept, in_specs=[hbm] * 9, out_specs=(vme...]
where the time goes in v3:
time: 24.5 us; the launch traced here: 24.4 us
  Pallas kernels  23.7 us (97%)
  between operations  0.64 us (3%)
    pallas_call x1, Pallas kernels, on_device(): pl.pallas_call(kernel, out_shape=kept, in_specs=[hbm] * 9, out_specs=(vme...  21.1 us
    pallas_call x1, Pallas kernels, on_device(): pl.pallas_call(last_kernel, out_shape=(jax.ShapeDtypeStruct((columns, 153...  2.62 us

profile of v3, /device:TPU:1, one launch (start us, length us, event | category | flops | bytes accessed | tf_op | source)
XLA Modules:
  0.0 24.4 jit_solution(5099941463076092050)
XLA Ops:
  0.6 21.1 %shard_map.112 = (f32[128,1536]{1,0:T(8,128)S(1)}, f32[128,1536]{1,0:T(8,128)S(1)}, f32[256,128]{1,0:T(8,128)S(1)}, bf16[32,256,256]{2,1,0:T(8,128)(2,1)S(1)}, f...) custom-call(f32[128,1536]{1,0:T(8,128)} %bitcast.7, f32[128,1536]{1,0:T(8,128)} %bitcast.8, f32[128,256]{1,0:T(8,128)} %bitcast.10, ...), custom_call_target="tpu_custom_call" | custom-call | tf_op jit(solution)/shard_map/pallas_call | solution.py:484
  21.7 2.6 %shard_map.113 = (f32[128,1536]{1,0:T(8,128)}, f32[128,1536]{1,0:T(8,128)}, f32[768,128]{1,0:T(8,128)}) custom-call(f32[128,1536]{1,0:T(8,128)S(1)} %get-tuple-element.12.u, f32[128,1536]{1,0:T(8,128)S(1)} %get-tuple-element.13.r, f32[256,128]{1,0:T(8,128)S(1)} %get-tuple-element.14.tb1, bf16[32,256,256]{2,1,0:T(8,128)(2,1)S(1)} %get-tuple-element.15.oh, ...), custom_call_target="tpu_custom_call" | custom-call | tf_op jit(solution)/shard_map/pallas_call | solution.py:529

commit v4 on v3

--- a/solution.py
+++ b/solution.py
@@ -84,7 +84,7 @@
     return high, (value - high.astype(F32)).astype(BF16)
 
 
-def interpolate(table, tt, oh, wt, pls):
+def interpolate(table, tt, oh, wt, pls, done=None):
     high, low = split2(table.T)
     tt[0:128] = high
     tt[128:256] = low
@@ -101,7 +101,12 @@
             pls[pl.ds(2 * pp + h, 8, stride=64), :] = total
         return carry
 
-    lax.fori_loop(0, 32, rows_of, 0, unroll=8)
+    if done is None:
+        lax.fori_loop(0, 32, rows_of, 0, unroll=8)
+    else:
+        for q in range(4):
+            lax.fori_loop(8 * q, 8 * q + 8, rows_of, 0, unroll=8)
+            done(q)
 
 
 def last_kernel(
@@ -111,12 +116,22 @@
         pltpu.make_async_copy(u, f_out, out_sem.at[0]),
         pltpu.make_async_copy(r, r_out, out_sem.at[1]),
         pltpu.make_async_copy(pls0.at[pl.ds(0, 384)], pl_out.at[pl.ds(0, 384)], out_sem.at[2]),
-        pltpu.make_async_copy(pls1.at[pl.ds(0, 384)], pl_out.at[pl.ds(384, 384)], out_sem.at[3]),
+    ] + [
+        pltpu.make_async_copy(
+            pls1.at[pl.ds(64 * c + 16 * q, 16)],
+            pl_out.at[pl.ds(384 + 64 * c + 16 * q, 16)],
+            out_sem.at[3 + 6 * q + c],
+        )
+        for q in range(4)
+        for c in range(6)
     ]
     for store in stores[:3]:
         store.start()
-    interpolate(tb1[...], tt, oh, wt, pls1)
-    stores[3].start()
+    def done(q):
+        for store in stores[3 + 6 * q : 9 + 6 * q]:
+            store.start()
+
+    interpolate(tb1[...], tt, oh, wt, pls1, done)
     for store in stores:
         store.wait()
 
@@ -125,7 +140,7 @@
     f_in, r_in, p_in, m_in, rt_in, st_in, co_in, w1_in, w2_in,
     u, r, tb1, oh, wt, pls,
     ep, me, rt, st, co, w1, w2,
-    gxb, gyb, hys, hyr, qz, xs, rr, pay, og, tb0, tt,
+    gxb, gyb, hys, hxr, hyr, qz, xs, rr, pay, og, tb0, tt,
     in_sem, hs_sem, hr_sem, sd_sem, rd_sem, ready,
 ):
     tb = (tb0, tb1)
@@ -139,8 +154,7 @@
              (p_in, ep), (st_in, st), (co_in, co)]
         )
     ]
-    for load in loads:
-        load.start()
+    loads[0].start()
 
     barrier = pltpu.get_barrier_semaphore()
 
@@ -154,6 +168,8 @@
 
     lax.fori_loop(1, NX, greet_x, 0)
     lax.fori_loop(1, NY, greet_y, 0)
+    for load in loads[1:]:
+        load.start()
 
     lane = lane_iota(CH)
     digit = [node_digit(a, lane) for a in range(3)]
@@ -231,8 +247,8 @@
         below = {"x": lax.rem(ix + NX - 1, NX), "y": lax.rem(iy + NY - 1, NY)}
         above = {"x": lax.rem(ix + 1, NX), "y": lax.rem(iy + 1, NY)}
         plan = [
-            (gxb.at[sec, :, pl.ds(8, 8)], gxb.at[sec, :, pl.ds(136, 8)], (below["x"], iy)),
-            (gxb.at[sec, :, pl.ds(128, 8)], gxb.at[sec, :, pl.ds(0, 8)], (above["x"], iy)),
+            (gxb.at[sec, :, pl.ds(8, 8)], hxr.at[sec, 0], (below["x"], iy)),
+            (gxb.at[sec, :, pl.ds(128, 8)], hxr.at[sec, 1], (above["x"], iy)),
             (hys.at[sec, 0], hyr.at[sec, 0], (ix, below["y"])),
             (hys.at[sec, 1], hyr.at[sec, 1], (ix, above["y"])),
         ]
@@ -251,23 +267,77 @@
         for copy in halo_copies(sec):
             copy.start()
 
+    above_is = [
+        jnp.where(ix == NX - 1, 0.0, 1.0).astype(F32), jnp.where(iy == NY - 1, 0.0, 1.0).astype(F32)
+    ]
+    below_is = [jnp.where(ix == 0, 0.0, 1.0).astype(F32), jnp.where(iy == 0, 0.0, 1.0).astype(F32)]
+
+    def beside_y(sec, k, xt):
+        up, down = (
+            jnp.concatenate(
+                [gyb[sec, k, pl.ds(2 * xt + at, 8), :], gyb[sec, k, pl.ds(2 * xt + at + 16, 8), :]],
+                axis=0,
+            )
+            for at in (9, 7)
+        )
+        return jnp.where(is3[1], up, down)
+
+    def no_halo(sec):
+        none = jnp.zeros((16, 128), F32)
+        for k in range(4):
+            gxb[sec, k, 136:144, :] = none[0:8]
+            gxb[sec, k, 0:8, :] = none[0:8]
+            gyb[sec, k, pl.ds(16, 16, stride=16), :] = none
+            gyb[sec, k, pl.ds(7, 16, stride=16), :] = none
+
     def take_halo(sec):
         for copy in halo_copies(sec):
             copy.wait_recv()
-
-        @pl.when(ix == NX - 1)
-        def _():
-            gxb[sec, :, 136:144, :] = jnp.zeros((4, 8, 128), F32)
-
-        @pl.when(ix == 0)
-        def _():
-            gxb[sec, :, 0:8, :] = jnp.zeros((4, 8, 128), F32)
-
-        has_up = jnp.where(iy == NY - 1, 0.0, 1.0).astype(F32)
-        has_down = jnp.where(iy == 0, 0.0, 1.0).astype(F32)
         for k in range(4):
-            gyb[sec, k, pl.ds(16, 16, stride=16), :] = hyr[sec, 0, k] * has_up
-            gyb[sec, k, pl.ds(7, 16, stride=16), :] = hyr[sec, 1, k] * has_down
+            gxb[sec, k, 136:144, :] = hxr[sec, 0, k] * above_is[0]
+            gxb[sec, k, 0:8, :] = hxr[sec, 1, k] * below_is[0]
+            gyb[sec, k, pl.ds(16, 16, stride=16), :] = hyr[sec, 0, k] * above_is[1]
+            gyb[sec, k, pl.ds(7, 16, stride=16), :] = hyr[sec, 1, k] * below_is[1]
+
+    def add_halo(sec):
+        take_halo(sec)
+
+        def share(rows, a, lp, mask, sign, values):
+            b, c = (a + 1) % 3, (a + 2) % 3
+            met = me[rows, (a * 2 + lp) * 128 : (a * 2 + lp + 1) * 128] * mask
+            scale = time_step / ep[rows, lp * 128 : (lp + 1) * 128]
+            for pair, e_comp, h_comp in ((0, b, c + 3), (1, c, b + 3)):
+                flux = met * values[pair]
+                turned = flux * (-sign if pair == 0 else sign)
+                for comp, rate in ((e_comp, flux * scale), (h_comp, turned)):
+                    cols = slice((comp * 2 + lp) * 128, (comp * 2 + lp + 1) * 128)
+                    r[rows, cols] += rate
+                    u[rows, cols] += section_gain[sec] * rate
+
+        for side in range(2):
+            rows = pl.ds(120 * side, 8)
+            mask = jnp.where(node_digit(0, lane_iota(8)) == 3 * side, lift_factor, 0.0)
+            sign = time_step * (2.0 * side - 1.0)
+            for lp in range(2):
+                share(
+                    rows, 0, lp, mask, sign,
+                    [gxb[sec, pair * 2 + lp, 136 * side : 136 * side + 8, :] for pair in range(2)],
+                )
+        col_y = lax.broadcasted_iota(jnp.int32, (CH, 128), 0) & 7
+        edge = ((digit[1] == 0) & (col_y == 0)) | (is3[1] & (col_y == 7))
+        mask = jnp.where(edge, lift_factor, 0.0)
+        sign = time_step * sg[1]
+
+        def rows_y(ch, carry):
+            r0 = pl.multiple_of(ch * CH, CH)
+            for lp in range(2):
+                share(
+                    pl.ds(r0, CH), 1, lp, mask, sign,
+                    [beside_y(sec, pair * 2 + lp, r0) for pair in range(2)],
+                )
+            return carry
+
+        lax.fori_loop(0, 128 // CH, rows_y, 0, unroll=8)
 
     def products():
         def one(g, carry):
@@ -276,7 +346,7 @@
             )
             return carry
 
-        lax.fori_loop(0, 3, one, 0)
+        lax.fori_loop(0, 3, one, 0, unroll=3)
 
     def finish(sec, r0):
         xt = pl.multiple_of(r0, CH)
@@ -310,15 +380,7 @@
                             )
                         )
                     elif a == 1:
-                        up = jnp.concatenate(
-                            [gyb[sec, k, pl.ds(2 * xt + 9, 8), :], gyb[sec, k, pl.ds(2 * xt + 25, 8), :]],
-                            axis=0,
-                        )
-                        down = jnp.concatenate(
-                            [gyb[sec, k, pl.ds(2 * xt + 7, 8), :], gyb[sec, k, pl.ds(2 * xt + 23, 8), :]],
-                            axis=0,
-                        )
-                        q.append(jnp.where(is3[1], up, down))
+                        q.append(beside_y(sec, k, xt))
                     else:
                         q.append(qz[k, rows, :])
                 add(b, met * (bd3[a] * (q[0] - val[b]) - slope(c + 3, a)))
@@ -394,7 +456,7 @@
         trace_rows(pl.multiple_of(r0, CH), ee, hh)
         return carry
 
-    lax.fori_loop(0, 128 // CH, first_faces, 0)
+    lax.fori_loop(0, 128 // CH, first_faces, 0, unroll=2)
 
     targets = jnp.broadcast_to(rt[...], (128, 128))
     earlier = lax.broadcasted_iota(jnp.int32, (128, 128), 0) < lane_iota(128)
@@ -411,13 +473,40 @@
     lax.fori_loop(1, NY, tell, 0)
     place(0)
 
-    loads[2].wait()
-    loads[3].wait()
+    no_halo(0)
+    for load in loads[2:7]:
+        load.wait()
     products()
 
-    for load in loads[4:]:
-        load.wait()
-
+    def own_section(ch, carry):
+        finish(0, ch * CH)
+        return carry
+
+    lax.fori_loop(0, 128 // CH, own_section, 0, unroll=4)
+    pl.semaphore_wait(ready, NY - 1)
+    send_traces(0)
+    add_halo(0)
+
+    def second_traces(ch, carry):
+        r0 = pl.multiple_of(ch * CH, CH)
+        both = tiles(u, r0)
+        trace_rows(r0, [both[lp][0:3] for lp in range(2)], [both[lp][3:6] for lp in range(2)])
+        return carry
+
+    lax.fori_loop(0, 128 // CH, second_traces, 0, unroll=8)
+    place(1)
+    send_traces(1)
+
+    def second_faces(ch, carry):
+        both = tiles(u, pl.multiple_of(ch * CH, CH))
+        faces(1, ch * CH, [both[lp][0:3] for lp in range(2)], [both[lp][3:6] for lp in range(2)])
+        return carry
+
+    lax.fori_loop(0, 128 // CH, second_faces, 0, unroll=2)
+    send_halo(1)
+
+    loads[7].wait()
+    loads[8].wait()
     along_u = basis(co[0])
     along_v = basis(co[1])
     for i in range(4):
@@ -431,25 +520,7 @@
             oh[pp, :, h * 128 : h * 128 + 128] = jnp.where(slot_iota == row, 1.0, 0.0).astype(BF16)
         return carry
 
-    lax.fori_loop(0, 32, one_hot, 0)
-
-    pl.semaphore_wait(ready, NY - 1)
-    send_traces(0)
-    take_halo(0)
-
-    def first_section(ch, carry):
-        r0 = ch * CH
-        new = finish(0, r0)
-        ee = [new[lp][0:3] for lp in range(2)]
-        hh = [new[lp][3:6] for lp in range(2)]
-        faces(1, r0, ee, hh)
-        trace_rows(pl.multiple_of(r0, CH), ee, hh)
-        return carry
-
-    lax.fori_loop(0, 128 // CH, first_section, 0)
-    place(1)
-    send_traces(1)
-    send_halo(1)
+    lax.fori_loop(0, 32, one_hot, 0, unroll=4)
     products()
     all_straight(0).wait_recv()
     interpolate(tb0[...], tt, oh, wt, pls)
@@ -459,7 +530,7 @@
         finish(1, ch * CH)
         return carry
 
-    lax.fori_loop(0, 128 // CH, second_section, 0)
+    lax.fori_loop(0, 128 // CH, second_section, 0, unroll=2)
     all_straight(1).wait_recv()
     for sec in range(2):
         for copy in halo_copies(sec):
@@ -497,6 +568,7 @@
             pltpu.VMEM((2, 4, 144, 128), F32),
             pltpu.VMEM((2, 4, 272, 128), F32),
             pltpu.VMEM((2, 2, 4, 16, 128), F32),
+            pltpu.VMEM((2, 2, 4, 8, 128), F32),
             pltpu.VMEM((2, 2, 4, 16, 128), F32),
             pltpu.VMEM((4, 128, 128), F32),
             pltpu.VMEM((3, 512, 256), BF16),
@@ -535,7 +607,7 @@
         ),
         in_specs=[vmem] * len(kept),
         out_specs=(hbm,) * 3,
-        scratch_shapes=[pltpu.VMEM((512, 128), F32), pltpu.VMEM((256, 256), BF16), dma((4,))],
+        scratch_shapes=[pltpu.VMEM((512, 128), F32), pltpu.VMEM((256, 256), BF16), dma((27,))],
         compiler_params=pltpu.CompilerParams(vmem_limit_bytes=VMEM_B * 1024 * 1024),
     )(*held)
     return (

time: 24.5 us -> 22.8 us (0.931)
  Pallas kernels: 23.7 us -> 22.1 us
    pallas_call x1, Pallas kernels: 21.1 us -> 19.9 us  [on_device(): pl.pallas_call(kernel, out_shape=kept, in_specs=[hbm] * 9, out_specs=(vme...]
    pallas_call x1, Pallas kernels: 2.62 us -> 2.17 us  [on_device(): pl.pallas_call(last_kernel, out_shape=(jax.ShapeDtypeStruct((columns, 153...]
where the time goes in v4:
time: 22.8 us; the launch traced here: 22.7 us
  Pallas kernels  22.1 us (97%)
  between operations  0.64 us (3%)
    pallas_call x1, Pallas kernels, on_device(): pl.pallas_call(kernel, out_shape=kept, in_specs=[hbm] * 9, out_specs=(vme...  19.9 us
    pallas_call x1, Pallas kernels, on_device(): pl.pallas_call(last_kernel, out_shape=(jax.ShapeDtypeStruct((columns, 153...  2.17 us

profile of v4, /device:TPU:1, one launch (start us, length us, event | category | flops | bytes accessed | tf_op | source)
XLA Modules:
  0.0 22.7 jit_solution(16722546449742715192)
XLA Ops:
  0.6 19.9 %shard_map.112 = (f32[128,1536]{1,0:T(8,128)S(1)}, f32[128,1536]{1,0:T(8,128)S(1)}, f32[256,128]{1,0:T(8,128)S(1)}, bf16[32,256,256]{2,1,0:T(8,128)(2,1)S(1)}, f...) custom-call(f32[128,1536]{1,0:T(8,128)} %bitcast.7, f32[128,1536]{1,0:T(8,128)} %bitcast.8, f32[128,256]{1,0:T(8,128)} %bitcast.10, ...), custom_call_target="tpu_custom_call" | custom-call | tf_op jit(solution)/shard_map/pallas_call | solution.py:555
  20.5 2.2 %shard_map.113 = (f32[128,1536]{1,0:T(8,128)}, f32[128,1536]{1,0:T(8,128)}, f32[768,128]{1,0:T(8,128)}) custom-call(f32[128,1536]{1,0:T(8,128)S(1)} %get-tuple-element.12.u, f32[128,1536]{1,0:T(8,128)S(1)} %get-tuple-element.13.r, f32[256,128]{1,0:T(8,128)S(1)} %get-tuple-element.14.tb1, bf16[32,256,256]{2,1,0:T(8,128)(2,1)S(1)} %get-tuple-element.15.oh, ...), custom_call_target="tpu_custom_call" | custom-call | tf_op jit(solution)/shard_map/pallas_call | solution.py:601

commit v5 on v4

--- a/solution.py
+++ b/solution.py
@@ -140,7 +140,7 @@
     f_in, r_in, p_in, m_in, rt_in, st_in, co_in, w1_in, w2_in,
     u, r, tb1, oh, wt, pls,
     ep, me, rt, st, co, w1, w2,
-    gxb, gyb, hys, hxr, hyr, qz, xs, rr, pay, og, tb0, tt,
+    gxb, gyb, hys, hxr, hyr, qz, xs, rr, pay, og, tb0, tt, put,
     in_sem, hs_sem, hr_sem, sd_sem, rd_sem, ready,
 ):
     tb = (tb0, tb1)
@@ -154,8 +154,6 @@
              (p_in, ep), (st_in, st), (co_in, co)]
         )
     ]
-    loads[0].start()
-
     barrier = pltpu.get_barrier_semaphore()
 
     def greet_x(d, carry):
@@ -166,9 +164,9 @@
         pl.semaphore_signal(barrier, inc=1, device_id=(ix, lax.rem(iy + d, NY)), device_id_type=MESH)
         return carry
 
-    lax.fori_loop(1, NX, greet_x, 0)
-    lax.fori_loop(1, NY, greet_y, 0)
-    for load in loads[1:]:
+    lax.fori_loop(1, NX, greet_x, 0, unroll=15)
+    lax.fori_loop(1, NY, greet_y, 0, unroll=7)
+    for load in loads:
         load.start()
 
     lane = lane_iota(CH)
@@ -261,10 +259,13 @@
         ]
 
     def send_halo(sec):
+        copies = halo_copies(sec)
+        for copy in copies[:2]:
+            copy.start()
         for k in range(4):
             hys[sec, 0, k] = gyb[sec, k, pl.ds(8, 16, stride=16), :]
             hys[sec, 1, k] = gyb[sec, k, pl.ds(15, 16, stride=16), :]
-        for copy in halo_copies(sec):
+        for copy in copies[2:]:
             copy.start()
 
     above_is = [
@@ -299,9 +300,7 @@
             gyb[sec, k, pl.ds(16, 16, stride=16), :] = hyr[sec, 0, k] * above_is[1]
             gyb[sec, k, pl.ds(7, 16, stride=16), :] = hyr[sec, 1, k] * below_is[1]
 
-    def add_halo(sec):
-        take_halo(sec)
-
+    def add_halo(sec, lp):
         def share(rows, a, lp, mask, sign, values):
             b, c = (a + 1) % 3, (a + 2) % 3
             met = me[rows, (a * 2 + lp) * 128 : (a * 2 + lp + 1) * 128] * mask
@@ -318,11 +317,10 @@
             rows = pl.ds(120 * side, 8)
             mask = jnp.where(node_digit(0, lane_iota(8)) == 3 * side, lift_factor, 0.0)
             sign = time_step * (2.0 * side - 1.0)
-            for lp in range(2):
-                share(
-                    rows, 0, lp, mask, sign,
-                    [gxb[sec, pair * 2 + lp, 136 * side : 136 * side + 8, :] for pair in range(2)],
-                )
+            share(
+                rows, 0, lp, mask, sign,
+                [gxb[sec, pair * 2 + lp, 136 * side : 136 * side + 8, :] for pair in range(2)],
+            )
         col_y = lax.broadcasted_iota(jnp.int32, (CH, 128), 0) & 7
         edge = ((digit[1] == 0) & (col_y == 0)) | (is3[1] & (col_y == 7))
         mask = jnp.where(edge, lift_factor, 0.0)
@@ -330,11 +328,10 @@
 
         def rows_y(ch, carry):
             r0 = pl.multiple_of(ch * CH, CH)
-            for lp in range(2):
-                share(
-                    pl.ds(r0, CH), 1, lp, mask, sign,
-                    [beside_y(sec, pair * 2 + lp, r0) for pair in range(2)],
-                )
+            share(
+                pl.ds(r0, CH), 1, lp, mask, sign,
+                [beside_y(sec, pair * 2 + lp, r0) for pair in range(2)],
+            )
             return carry
 
         lax.fori_loop(0, 128 // CH, rows_y, 0, unroll=8)
@@ -432,17 +429,13 @@
 
     def place(sample):
         value = pay[...]
-        high, rest = value.astype(BF16), None
+        high = value.astype(BF16)
         rest = value - high.astype(F32)
         mid = rest.astype(BF16)
         low = (rest - mid.astype(F32)).astype(BF16)
-        slot = jnp.broadcast_to(slots, (256, 128))
-        where = lax.broadcasted_iota(jnp.int32, (256, 128), 0) == slot
-        put = jnp.where(where, 1.0, 0.0).astype(BF16)
-        og[sample] = (
-            jnp.dot(put, high, preferred_element_type=F32)
-            + jnp.dot(put, mid, preferred_element_type=F32)
-        ) + jnp.dot(put, low, preferred_element_type=F32)
+        og[sample] = jnp.dot(
+            put[...], jnp.concatenate([high, mid, low], axis=0), preferred_element_type=F32
+        )
 
     loads[0].wait()
     loads[1].wait()
@@ -462,6 +455,9 @@
     earlier = lax.broadcasted_iota(jnp.int32, (128, 128), 0) < lane_iota(128)
     same = jnp.where((targets.T == targets) & earlier, 1, 0)
     slots = rt[...] * 2 + jnp.sum(same, axis=0, keepdims=True)
+    where = lax.broadcasted_iota(jnp.int32, (256, 128), 0) == jnp.broadcast_to(slots, (256, 128))
+    for n in range(3):
+        put[:, n * 128 : n * 128 + 128] = jnp.where(where, 1.0, 0.0).astype(BF16)
 
     pl.semaphore_wait(barrier, NX - 1 + NY - 1)
     send_halo(0)
@@ -470,7 +466,7 @@
         pl.semaphore_signal(ready, inc=1, device_id=(ix, lax.rem(iy + d, NY)), device_id_type=MESH)
         return carry
 
-    lax.fori_loop(1, NY, tell, 0)
+    lax.fori_loop(1, NY, tell, 0, unroll=7)
     place(0)
 
     no_halo(0)
@@ -485,7 +481,8 @@
     lax.fori_loop(0, 128 // CH, own_section, 0, unroll=4)
     pl.semaphore_wait(ready, NY - 1)
     send_traces(0)
-    add_halo(0)
+    take_halo(0)
+    add_halo(0, 1)
 
     def second_traces(ch, carry):
         r0 = pl.multiple_of(ch * CH, CH)
@@ -496,6 +493,7 @@
     lax.fori_loop(0, 128 // CH, second_traces, 0, unroll=8)
     place(1)
     send_traces(1)
+    add_halo(0, 0)
 
     def second_faces(ch, carry):
         both = tiles(u, pl.multiple_of(ch * CH, CH))
@@ -577,6 +575,7 @@
             pltpu.VMEM((2, 256, 128), F32),
             pltpu.VMEM((256, 128), F32),
             pltpu.VMEM((256, 256), BF16),
+            pltpu.VMEM((256, 384), BF16),
             dma((9,)),
             dma((2, 4)),
             dma((2, 4)),

time: 22.8 us -> 22.7 us (level)
  no operation moved by 1% of the time
where the time goes in v5:
time: 22.7 us; the launch traced here: 22.6 us
  Pallas kernels  22 us (97%)
  between operations  0.64 us (3%)
    pallas_call x1, Pallas kernels, on_device(): pl.pallas_call(kernel, out_shape=kept, in_specs=[hbm] * 9, out_specs=(vme...  19.8 us
    pallas_call x1, Pallas kernels, on_device(): pl.pallas_call(last_kernel, out_shape=(jax.ShapeDtypeStruct((columns, 153...  2.17 us

profile of v5, /device:TPU:1, one launch (start us, length us, event | category | flops | bytes accessed | tf_op | source)
XLA Modules:
  0.0 22.6 jit_solution(1574091194671171432)
XLA Ops:
  0.6 19.8 %shard_map.112 = (f32[128,1536]{1,0:T(8,128)S(1)}, f32[128,1536]{1,0:T(8,128)S(1)}, f32[256,128]{1,0:T(8,128)S(1)}, bf16[32,256,256]{2,1,0:T(8,128)(2,1)S(1)}, f...) custom-call(f32[128,1536]{1,0:T(8,128)} %bitcast.7, f32[128,1536]{1,0:T(8,128)} %bitcast.8, f32[128,256]{1,0:T(8,128)} %bitcast.10, ...), custom_call_target="tpu_custom_call" | custom-call | tf_op jit(solution)/shard_map/pallas_call | solution.py:553
  20.4 2.2 %shard_map.113 = (f32[128,1536]{1,0:T(8,128)}, f32[128,1536]{1,0:T(8,128)}, f32[768,128]{1,0:T(8,128)}) custom-call(f32[128,1536]{1,0:T(8,128)S(1)} %get-tuple-element.12.u, f32[128,1536]{1,0:T(8,128)S(1)} %get-tuple-element.13.r, f32[256,128]{1,0:T(8,128)S(1)} %get-tuple-element.14.tb1, bf16[32,256,256]{2,1,0:T(8,128)(2,1)S(1)} %get-tuple-element.15.oh, ...), custom_call_target="tpu_custom_call" | custom-call | tf_op jit(solution)/shard_map/pallas_call | solution.py:600

commit v6 on v5

--- a/solution.py
+++ b/solution.py
@@ -84,10 +84,13 @@
     return high, (value - high.astype(F32)).astype(BF16)
 
 
-def interpolate(table, tt, oh, wt, pls, done=None):
-    high, low = split2(table.T)
-    tt[0:128] = high
-    tt[128:256] = low
+def interpolate(table, cmat, tt, oh, wt, pls, done=None):
+    used = lax.dot_general(
+        jnp.concatenate(split2(table.T), axis=0), cmat[...], (((1,), (1,)), ((), ())),
+        preferred_element_type=F32,
+    )
+    tt[:, 0:128] = used[0:128].astype(BF16)
+    tt[:, 128:256] = used[128:256].astype(BF16)
 
     def rows_of(pp, carry):
         got = jnp.dot(tt[...], oh[pp], preferred_element_type=F32)
@@ -95,7 +98,7 @@
             part = got[:, h * 128 : h * 128 + 128]
             total = None
             for n in range(16):
-                both = part[n * 8 : n * 8 + 8] + part[128 + n * 8 : 136 + n * 8]
+                both = part[n * 8 : n * 8 + 8]
                 term = both * wt[n, pl.ds(2 * pp + h, 1), :]
                 total = term if total is None else total + term
             pls[pl.ds(2 * pp + h, 8, stride=64), :] = total
@@ -110,7 +113,7 @@
 
 
 def last_kernel(
-    u, r, tb1, oh, wt, pls0, f_out, r_out, pl_out, pls1, tt, out_sem
+    u, r, tb1, cmat, oh, wt, pls0, f_out, r_out, pl_out, pls1, tt, out_sem
 ):
     stores = [
         pltpu.make_async_copy(u, f_out, out_sem.at[0]),
@@ -131,14 +134,14 @@
         for store in stores[3 + 6 * q : 9 + 6 * q]:
             store.start()
 
-    interpolate(tb1[...], tt, oh, wt, pls1, done)
+    interpolate(tb1[...], cmat, tt, oh, wt, pls1, done)
     for store in stores:
         store.wait()
 
 
 def kernel(
     f_in, r_in, p_in, m_in, rt_in, st_in, co_in, w1_in, w2_in,
-    u, r, tb1, oh, wt, pls,
+    u, r, tb1, cmat, oh, wt, pls,
     ep, me, rt, st, co, w1, w2,
     gxb, gyb, hys, hxr, hyr, qz, xs, rr, pay, og, tb0, tt, put,
     in_sem, hs_sem, hr_sem, sd_sem, rd_sem, ready,
@@ -229,7 +232,7 @@
                     xs[g, rows, 128:256] = low
 
     def trace_rows(r0, ee, hh):
-        total = jnp.zeros((CH, 128), F32)
+        total = jnp.where(lane == 6, 1.0, 0.0).astype(F32)
         for c in range(6):
             side = ee if c < 3 else hh
             total = jnp.where(comp_lane == c, permute(side[1][c % 3], pick), total)
@@ -510,18 +513,31 @@
     for i in range(4):
         for j in range(4):
             wt[i * 4 + j] = along_u[i] * along_v[j]
-    slot_iota = lax.broadcasted_iota(jnp.int32, (256, 128), 0)
+    products()
+    all_straight(0).wait_recv()
+
+    used = tb0[...].T[6:7]
+    before = lax.broadcasted_iota(jnp.int32, (256, 256), 0) < lax.broadcasted_iota(jnp.int32, (256, 256), 1)
+    place_of = jnp.dot(
+        jnp.broadcast_to(used, (8, 256)).astype(BF16), jnp.where(before, 1.0, 0.0).astype(BF16),
+        preferred_element_type=F32,
+    )[0:1]
+    index = lax.broadcasted_iota(jnp.int32, (128, 256), 0).astype(F32)
+    chosen = jnp.where(index == jnp.broadcast_to(place_of, (128, 256)), 1.0, 0.0)
+    cmat[...] = (chosen * used).astype(BF16)
+    row_ids = lax.broadcasted_iota(jnp.int32, (256, 128), 0).astype(F32).astype(BF16)
+    ids = jnp.dot(cmat[...], row_ids, preferred_element_type=F32)
 
     def one_hot(pp, carry):
         for h in range(2):
-            row = jnp.broadcast_to(st[pl.ds(2 * pp + h, 1), :], (256, 128))
-            oh[pp, :, h * 128 : h * 128 + 128] = jnp.where(slot_iota == row, 1.0, 0.0).astype(BF16)
+            row = jnp.broadcast_to(st[pl.ds(2 * pp + h, 1), :].astype(F32), (128, 128))
+            match = jnp.where(ids == row, 1.0, 0.0).astype(BF16)
+            oh[pp, 0:128, h * 128 : h * 128 + 128] = match
+            oh[pp, 128:256, h * 128 : h * 128 + 128] = match
         return carry
 
     lax.fori_loop(0, 32, one_hot, 0, unroll=4)
-    products()
-    all_straight(0).wait_recv()
-    interpolate(tb0[...], tt, oh, wt, pls)
+    interpolate(tb0[...], cmat, tt, oh, wt, pls)
     take_halo(1)
 
     def second_section(ch, carry):
@@ -546,6 +562,7 @@
         pltpu.VMEM((128, 1536), F32),
         pltpu.VMEM((128, 1536), F32),
         pltpu.VMEM((256, 128), F32),
+        pltpu.VMEM((128, 256), BF16),
         pltpu.VMEM((32, 256, 256), BF16),
         pltpu.VMEM((16, 64, 128), F32),
         pltpu.VMEM((512, 128), F32),
@@ -574,7 +591,7 @@
             pltpu.VMEM((128, 128), F32),
             pltpu.VMEM((2, 256, 128), F32),
             pltpu.VMEM((256, 128), F32),
-            pltpu.VMEM((256, 256), BF16),
+            pltpu.VMEM((128, 256), BF16),
             pltpu.VMEM((256, 384), BF16),
             dma((9,)),
             dma((2, 4)),
@@ -606,7 +623,7 @@
         ),
         in_specs=[vmem] * len(kept),
         out_specs=(hbm,) * 3,
-        scratch_shapes=[pltpu.VMEM((512, 128), F32), pltpu.VMEM((256, 256), BF16), dma((27,))],
+        scratch_shapes=[pltpu.VMEM((512, 128), F32), pltpu.VMEM((128, 256), BF16), dma((27,))],
         compiler_params=pltpu.CompilerParams(vmem_limit_bytes=VMEM_B * 1024 * 1024),
     )(*held)
     return (

time: 22.7 us -> 22.6 us (level)
  no operation moved by 1% of the time
where the time goes in v6:
time: 22.6 us; the launch traced here: 22.5 us
  Pallas kernels  21.8 us (96%)
  between operations  0.64 us (3%)
    pallas_call x1, Pallas kernels, on_device(): pl.pallas_call(kernel, out_shape=kept, in_specs=[hbm] * 9, out_specs=(vme...  19.8 us
    pallas_call x1, Pallas kernels, on_device(): pl.pallas_call(last_kernel, out_shape=(jax.ShapeDtypeStruct((columns, 153...  2.01 us

profile of v6, /device:TPU:1, one launch (start us, length us, event | category | flops | bytes accessed | tf_op | source)
XLA Modules:
  0.0 22.5 jit_solution(4117671671352113249)
XLA Ops:
  0.6 19.8 %shard_map.112 = (f32[128,1536]{1,0:T(8,128)S(1)}, f32[128,1536]{1,0:T(8,128)S(1)}, f32[256,128]{1,0:T(8,128)S(1)}, bf16[128,256]{1,0:T(8,128)(2,1)S(1)}, bf16[3...) custom-call(f32[128,1536]{1,0:T(8,128)} %bitcast.7, f32[128,1536]{1,0:T(8,128)} %bitcast.8, ...), custom_call_target="tpu_custom_call" | custom-call | tf_op jit(solution)/shard_map/pallas_call | solution.py:570
  20.4 2.0 %shard_map.113 = (f32[128,1536]{1,0:T(8,128)}, f32[128,1536]{1,0:T(8,128)}, f32[768,128]{1,0:T(8,128)}) custom-call(f32[128,1536]{1,0:T(8,128)S(1)} %get-tuple-element.13.u, f32[128,1536]{1,0:T(8,128)S(1)} %get-tuple-element.14.r, f32[256,128]{1,0:T(8,128)S(1)} %get-tuple-element.15.tb1, bf16[128,256]{1,0:T(8,128)(2,1)S(1)} %get-tuple-element.16.cmat, ...), custom_call_target="tpu_custom_call" | custom-call | tf_op jit(solution)/shard_map/pallas_call | solution.py:617

commit v7 on v5

--- a/solution.py
+++ b/solution.py
@@ -548,7 +548,7 @@
         pltpu.VMEM((256, 128), F32),
         pltpu.VMEM((32, 256, 256), BF16),
         pltpu.VMEM((16, 64, 128), F32),
-        pltpu.VMEM((512, 128), F32),
+        pltpu.VMEM((576, 128), F32),
     )
     held = pl.pallas_call(
         kernel,
@@ -606,7 +606,7 @@
         ),
         in_specs=[vmem] * len(kept),
         out_specs=(hbm,) * 3,
-        scratch_shapes=[pltpu.VMEM((512, 128), F32), pltpu.VMEM((256, 256), BF16), dma((27,))],
+        scratch_shapes=[pltpu.VMEM((576, 128), F32), pltpu.VMEM((256, 256), BF16), dma((27,))],
         compiler_params=pltpu.CompilerParams(vmem_limit_bytes=VMEM_B * 1024 * 1024),
     )(*held)
     return (

time: 22.7 us -> 22.7 us (level)
  no operation moved by 1% of the time
where the time goes in v7:
time: 22.7 us; the launch traced here: 22.6 us
  Pallas kernels  22 us (97%)
  between operations  0.64 us (3%)
    pallas_call x1, Pallas kernels, on_device(): pl.pallas_call(kernel, out_shape=kept, in_specs=[hbm] * 9, out_specs=(vme...  19.8 us
    pallas_call x1, Pallas kernels, on_device(): pl.pallas_call(last_kernel, out_shape=(jax.ShapeDtypeStruct((columns, 153...  2.17 us

profile of v7, /device:TPU:1, one launch (start us, length us, event | category | flops | bytes accessed | tf_op | source)
XLA Modules:
  0.0 22.6 jit_solution(1574091194671171432)
XLA Ops:
  0.6 19.8 %shard_map.112 = (f32[128,1536]{1,0:T(8,128)S(1)}, f32[128,1536]{1,0:T(8,128)S(1)}, f32[256,128]{1,0:T(8,128)S(1)}, bf16[32,256,256]{2,1,0:T(8,128)(2,1)S(1)}, f...) custom-call(f32[128,1536]{1,0:T(8,128)} %bitcast.7, f32[128,1536]{1,0:T(8,128)} %bitcast.8, f32[128,256]{1,0:T(8,128)} %bitcast.10, ...), custom_call_target="tpu_custom_call" | custom-call | tf_op jit(solution)/shard_map/pallas_call | solution.py:553
  20.4 2.2 %shard_map.113 = (f32[128,1536]{1,0:T(8,128)}, f32[128,1536]{1,0:T(8,128)}, f32[768,128]{1,0:T(8,128)}) custom-call(f32[128,1536]{1,0:T(8,128)S(1)} %get-tuple-element.12.u, f32[128,1536]{1,0:T(8,128)S(1)} %get-tuple-element.13.r, f32[256,128]{1,0:T(8,128)S(1)} %get-tuple-element.14.tb1, bf16[32,256,256]{2,1,0:T(8,128)(2,1)S(1)} %get-tuple-element.15.oh, ...), custom_call_target="tpu_custom_call" | custom-call | tf_op jit(solution)/shard_map/pallas_call | solution.py:600
